TPU v7x, 32 devices: a whole 2x2x4 slice. The times are simulated.
32 devices in a mesh: groups: 2 (over y), cable: 4 (over z), bins: 2 (over x), pairs: 2 (over core).
Axes of the slice: x: 2, y: 2, z: 4, core: 2. Of those that a mesh axis runs over, the one named last changes fastest.
Arguments:
- spectra: bfloat16 [4, 16, 256, 2048], P('groups', None, 'cable', 'bins'), parts along dimension 0, may hold values from -6 to 6
- counts: int32 [8], P(('groups', 'cable')), parts along dimension 0, may hold values from 1 to 4, as said below
- owners: int32 [8, 4], P(('groups', 'cable')), parts along dimension 0, may hold values from 0 to 1
Outputs:
- stacks: float32 [4, 4, 320, 2048], P('groups', 'cable', 'pairs', 'bins'), parts along dimension 0
There are 2 independent parts, one for each index of `groups`. A program takes and returns all parts, laid end to end along the dimension named above; each array names one. Nothing has to cross between parts.
Inputs may be any that keep to these rules, and one draw needn't show every extreme that they name: `counts`: block 0 keeps 4 offsets and block 1 keeps 1.
All inputs are finite; a program needn't handle non-finite values.
Results may differ from a plain program's by a relative error of at most 0.0017.
Values may be sent and summed in bfloat16 or wider, within the bound.
A program may use at most 128 MiB of HBM per device.

v0:
```python
import math

import jax
import jax.numpy as jnp
from jax import lax
from jax.sharding import PartitionSpec as P

REACH = 3
HALF_WIDTH = 32


epsilon = 1e-06
band_rows = 16


def with_halo(x, sides, width):
    for axis, dim in sides:
        count, length = (lax.axis_size(axis), x.shape[dim])
        up = [(i, (i + 1) % count) for i in range(count - 1)]
        down = [(j, i) for i, j in up]
        last = lax.slice_in_dim(x, length - width, length, axis=dim)
        first = lax.slice_in_dim(x, 0, width, axis=dim)
        before = lax.ppermute(last, axis, up)
        after = lax.ppermute(first, axis, down)
        x = jnp.concatenate([before, x, after], axis=dim)
    return x


def from_behind(block, axis, distance):
    devices = range(lax.axis_size(axis))
    route = [(i - distance, i) for i in devices if i - distance in devices]
    return lax.ppermute(block, axis, route)


def whiten_rows(spectra):
    real_part = spectra[0].astype(jnp.float32)
    imag_part = spectra[1].astype(jnp.float32)
    power_sum = real_part * real_part + imag_part * imag_part
    padded = with_halo(power_sum, (("bins", 2),), HALF_WIDTH)
    window_len = 2 * HALF_WIDTH + 1
    window_sum = lax.reduce_window(
        padded, jnp.zeros((), padded.dtype), lax.add, (1, 1, window_len), (1, 1, 1), "VALID"
    )
    inverse_amp = lax.rsqrt(window_sum / window_len + epsilon)
    return jnp.stack(
        [
            (real_part * inverse_amp).astype(jnp.bfloat16),
            (imag_part * inverse_amp).astype(jnp.bfloat16),
        ]
    )


def make_lag_table(col_count):
    flattened = jnp.arange(band_rows * col_count)
    row_of = flattened // col_count
    col_of = flattened % col_count
    lag_lanes = jnp.arange(col_count + band_rows - 1)
    return (lag_lanes[None, :] == (col_of - row_of + band_rows - 1)[:, None]).astype(jnp.bfloat16)


def lag_stack(pair_block, lag_table):
    freq_count, row_count, col_count = pair_block.shape
    group_count = row_count // band_rows
    grouped = pair_block.reshape(freq_count, group_count, band_rows * col_count)
    banded = jnp.einsum("fgk,ku->fgu", grouped, lag_table, preferred_element_type=jnp.float32)
    lag_sums = jnp.zeros((freq_count, col_count + row_count - 1), jnp.float32)
    for row_group in range(group_count):
        first_lag = row_count - band_rows * (row_group + 1)
        lag_sums = lag_sums.at[:, first_lag : first_lag + col_count + band_rows - 1].add(
            banded[:, row_group]
        )
    return lag_sums.T


def correlate(left_rows, right_rows, factor, lag_table):
    left_real = jnp.concatenate([left_rows[0], left_rows[1]], axis=0)
    left_imag = jnp.concatenate([left_rows[1], -left_rows[0]], axis=0)
    right_both = jnp.concatenate([right_rows[0], right_rows[1]], axis=0)
    corr_real = (
        jnp.einsum("wif,wjf->fij", left_real, right_both, preferred_element_type=jnp.float32)
        * factor
    ).astype(jnp.bfloat16)
    corr_imag = (
        jnp.einsum("wif,wjf->fij", left_imag, right_both, preferred_element_type=jnp.float32)
        * factor
    ).astype(jnp.bfloat16)
    return jnp.stack([lag_stack(corr_real, lag_table), lag_stack(corr_imag, lag_table)])


def shards(spectra, counts, owners):
    pair_devs = lax.axis_size("pairs")
    member = lax.axis_index("pairs")
    channels = spectra.shape[2]
    half_rows = channels // pair_devs
    source = whiten_rows(spectra)
    receiver = lax.dynamic_slice_in_dim(source, member * half_rows, half_rows, 2)
    block_count = lax.axis_size("cable")
    cable_index = lax.axis_index("cable")
    live_count = jnp.minimum(counts[0], block_count - cable_index)
    panels = {0: receiver}
    for offset in range(1, REACH + 1):
        panels[offset] = from_behind(receiver, "cable", -offset)
    factor = 1.0 / math.sqrt(source.shape[1] * channels)
    lag_table = make_lag_table(half_rows)
    freq_count = source.shape[3]
    stacks = jnp.zeros((2, (REACH + 2) * channels, freq_count), jnp.float32)
    for offset in range(REACH + 1):
        lag_piece = correlate(source, panels[offset], factor, lag_table)
        weight = (offset < live_count).astype(jnp.float32)
        if offset == 0:
            kept_here = weight * lag_piece
        else:
            sent_away = owners[0, offset].astype(jnp.float32)
            arrived = from_behind(weight * sent_away * lag_piece, "cable", offset)
            kept_here = weight * (1.0 - sent_away) * lag_piece + arrived
        first_lag = offset * channels + member * half_rows
        current = lax.dynamic_slice_in_dim(stacks, first_lag, kept_here.shape[1], 1)
        stacks = lax.dynamic_update_slice_in_dim(stacks, current + kept_here, first_lag, 1)
    summed = lax.psum_scatter(stacks, "pairs", scatter_dimension=1, tiled=True)
    return summed[:, None]


def solution(mesh):
    placed = (
        P("groups", None, "cable", "bins"),
        P(("groups", "cable")),
        P(("groups", "cable"), None),
    )
    return jax.shard_map(
        shards,
        mesh=mesh,
        in_specs=placed,
        out_specs=P("groups", "cable", "pairs", "bins"),
        check_vma=False,
    )
```

profile of v0, /device:TPU:0, one launch (start us, length us, event | category | flops | bytes accessed | tf_op | source)
XLA Modules:
  0.0 665.4 jit_solution(17789953391849906902)
XLA Ops:
  6.5 3.2 fusion.4
  12.2 4.9 collective-permute-start
  24.1 2.8 collective-permute-done.1
  27.1 6.4 concatenate.91
  33.5 148.7 %reduce_window.7 = f32[16,64,1024]{2,1,0:T(8,128)} reduce-window(f32[16,64,1088]{2,1,0:T(8,128)} %concatenate.91, f32[]{:T(128)} %constant.716.clone.1), window={size=1x1x65}, to_apply=%region_0.0 | reduce-window | flops 67108864 | bytes 8650756 | tf_op jit(solution)/shard_map/reduce_window | solution.py:41
  182.3 5.1 fusion.8
  190.4 2.5 fusion.50
  201.6 15.3 %copy.55 = bf16[32,32,1024]{0,1,2:T(8,128)(2,1)} copy(bf16[32,32,1024]{2,1,0:T(8,128)(2,1)} %pad_maximum_fusion.2) | data formatting | bytes 4194304 | tf_op jit(solution)/shard_map/concatenate | solution.py:78
  216.8 5.7 pad_maximum_fusion
  222.5 13.0 %copy.58 = bf16[32,64,1024]{1,0,2:T(8,128)(2,1)} copy(bf16[32,64,1024]{2,1,0:T(8,128)(2,1)} %get-tuple-element.402) | data formatting | bytes 8388608 | tf_op jit(solution)/shard_map/concatenate | solution.py:77
  235.5 11.4 %multiply_convert_fusion.6 = bf16[1024,64,32]{1,2,0:T(8,128)(2,1)} fusion(bf16[32,32,1024]{0,1,2:T(8,128)(2,1)} %copy.55, bf16[32,64,1024]{1,0,2:T(8,128)(2,1)} %copy.58), kind=kOutput, calls=%fused_computation.6 | convolution fusion | flops 138412032 | bytes 10485760 | tf_op jit(solution)/shard_map/wif,wjf->fij/dot_general | solution.py:84
  246.9 12.0 %copy.60 = bf16[1024,64,32]{0,2,1:T(8,128)(2,1)} copy(bf16[1024,64,32]{1,2,0:T(8,128)(2,1)} %multiply_convert_fusion.6) | data formatting | bytes 8388608 | tf_op jit(solution)/shard_map/convert_element_type | solution.py:86
  258.9 3.3 fusion.29
  262.3 12.9 %copy.54 = bf16[32,64,1024]{1,0,2:T(8,128)(2,1)} copy(bf16[32,64,1024]{2,1,0:T(8,128)(2,1)} %get-tuple-element.401) | data formatting | bytes 8388608 | tf_op jit(solution)/shard_map/concatenate | solution.py:76
  275.2 11.3 %multiply_convert_fusion.7 = bf16[1024,64,32]{1,2,0:T(8,128)(2,1)} fusion(bf16[32,32,1024]{0,1,2:T(8,128)(2,1)} %copy.55, bf16[32,64,1024]{1,0,2:T(8,128)(2,1)} %copy.54), kind=kOutput, calls=%fused_computation.7 | convolution fusion | flops 138412032 | bytes 10485760 | tf_op jit(solution)/shard_map/wif,wjf->fij/dot_general | solution.py:80
  286.5 12.2 %copy.56 = bf16[1024,64,32]{0,2,1:T(8,128)(2,1)} copy(bf16[1024,64,32]{1,2,0:T(8,128)(2,1)} %multiply_convert_fusion.7) | data formatting | bytes 8388608 | tf_op jit(solution)/shard_map/convert_element_type | solution.py:82
  298.7 3.3 fusion.31
  312.4 13.0 %copy.63 = bf16[32,32,1024]{0,1,2:T(8,128)(2,1)} copy(bf16[32,32,1024]{2,1,0:T(8,128)(2,1)S(1)} %pad_maximum_fusion.3) | data formatting | bytes 4194304 | tf_op jit(solution)/shard_map/concatenate | solution.py:78
  325.4 11.3 %multiply_convert_fusion.4 = bf16[1024,64,32]{1,2,0:T(8,128)(2,1)} fusion(bf16[32,32,1024]{0,1,2:T(8,128)(2,1)} %copy.63, bf16[32,64,1024]{1,0,2:T(8,128)(2,1)} %copy.58), kind=kOutput, calls=%fused_computation.4 | convolution fusion | flops 138412032 | bytes 10485760 | tf_op jit(solution)/shard_map/wif,wjf->fij/dot_general | solution.py:84
  336.7 12.1 %copy.68 = bf16[1024,64,32]{0,2,1:T(8,128)(2,1)} copy(bf16[1024,64,32]{1,2,0:T(8,128)(2,1)} %multiply_convert_fusion.4) | data formatting | bytes 8388608 | tf_op jit(solution)/shard_map/convert_element_type | solution.py:86
  348.7 3.3 fusion.25
  354.4 11.3 %multiply_convert_fusion.5 = bf16[1024,64,32]{1,2,0:T(8,128)(2,1)} fusion(bf16[32,32,1024]{0,1,2:T(8,128)(2,1)} %copy.63, bf16[32,64,1024]{1,0,2:T(8,128)(2,1)} %copy.54), kind=kOutput, calls=%fused_computation.5 | convolution fusion | flops 138412032 | bytes 10485760 | tf_op jit(solution)/shard_map/wif,wjf->fij/dot_general | solution.py:80
  365.7 12.2 %copy.64 = bf16[1024,64,32]{0,2,1:T(8,128)(2,1)} copy(bf16[1024,64,32]{1,2,0:T(8,128)(2,1)} %multiply_convert_fusion.5) | data formatting | bytes 8388608 | tf_op jit(solution)/shard_map/convert_element_type | solution.py:82
  377.9 3.3 fusion.27
  384.8 13.0 %copy.73 = bf16[32,32,1024]{0,1,2:T(8,128)(2,1)} copy(bf16[32,32,1024]{2,1,0:T(8,128)(2,1)S(1)} %pad_maximum_fusion.4) | data formatting | bytes 4194304 | tf_op jit(solution)/shard_map/concatenate | solution.py:78
  397.8 11.3 %multiply_convert_fusion.2 = bf16[1024,64,32]{1,2,0:T(8,128)(2,1)} fusion(bf16[32,32,1024]{0,1,2:T(8,128)(2,1)} %copy.73, bf16[32,64,1024]{1,0,2:T(8,128)(2,1)} %copy.58), kind=kOutput, calls=%fused_computation.2 | convolution fusion | flops 138412032 | bytes 10485760 | tf_op jit(solution)/shard_map/wif,wjf->fij/dot_general | solution.py:84
  409.1 12.1 %copy.78 = bf16[1024,64,32]{0,2,1:T(8,128)(2,1)} copy(bf16[1024,64,32]{1,2,0:T(8,128)(2,1)} %multiply_convert_fusion.2) | data formatting | bytes 8388608 | tf_op jit(solution)/shard_map/convert_element_type | solution.py:86
  421.2 3.3 fusion.21
  424.6 11.6 %multiply_convert_fusion.3 = bf16[1024,64,32]{1,2,0:T(8,128)(2,1)} fusion(bf16[32,32,1024]{0,1,2:T(8,128)(2,1)} %copy.73, bf16[32,64,1024]{1,0,2:T(8,128)(2,1)} %copy.54), kind=kOutput, calls=%fused_computation.3 | convolution fusion | flops 138412032 | bytes 10485760 | tf_op jit(solution)/shard_map/wif,wjf->fij/dot_general | solution.py:80
  436.1 12.4 %copy.74 = bf16[1024,64,32]{0,2,1:T(8,128)(2,1)} copy(bf16[1024,64,32]{1,2,0:T(8,128)(2,1)} %multiply_convert_fusion.3) | data formatting | bytes 8388608 | tf_op jit(solution)/shard_map/convert_element_type | solution.py:82
  448.6 3.4 fusion.23
  452.0 2.4 add_select_fusion.14
  457.8 12.9 %copy.83 = bf16[32,32,1024]{0,1,2:T(8,128)(2,1)} copy(bf16[32,32,1024]{2,1,0:T(8,128)(2,1)S(1)} %pad_maximum_fusion.5) | data formatting | bytes 4194304 | tf_op jit(solution)/shard_map/concatenate | solution.py:78
  470.6 11.4 %multiply_convert_fusion = bf16[1024,64,32]{1,2,0:T(8,128)(2,1)} fusion(bf16[32,32,1024]{0,1,2:T(8,128)(2,1)} %copy.83, bf16[32,64,1024]{1,0,2:T(8,128)(2,1)} %copy.58), kind=kOutput, calls=%fused_computation | convolution fusion | flops 138412032 | bytes 10485760 | tf_op jit(solution)/shard_map/wif,wjf->fij/dot_general | solution.py:84
  482.0 11.4 %multiply_convert_fusion.1 = bf16[1024,64,32]{1,2,0:T(8,128)(2,1)} fusion(bf16[32,32,1024]{0,1,2:T(8,128)(2,1)} %copy.83, bf16[32,64,1024]{1,0,2:T(8,128)(2,1)} %copy.54), kind=kOutput, calls=%fused_computation.1 | convolution fusion | flops 138412032 | bytes 10485760 | tf_op jit(solution)/shard_map/wif,wjf->fij/dot_general | solution.py:80
  493.4 12.0 %copy.88 = bf16[1024,64,32]{0,2,1:T(8,128)(2,1)} copy(bf16[1024,64,32]{1,2,0:T(8,128)(2,1)} %multiply_convert_fusion) | data formatting | bytes 8388608 | tf_op jit(solution)/shard_map/convert_element_type | solution.py:86
  505.4 3.3 fusion.17
  509.7 12.0 %copy.84 = bf16[1024,64,32]{0,2,1:T(8,128)(2,1)} copy(bf16[1024,64,32]{1,2,0:T(8,128)(2,1)} %multiply_convert_fusion.1) | data formatting | bytes 8388608 | tf_op jit(solution)/shard_map/convert_element_type | solution.py:82
  521.8 3.4 fusion.19
  542.5 2.3 add_select_fusion.15
  548.4 30.8 %collective-permute-start.3 = (f32[2,95,1024]{2,0,1:T(2,128)}, f32[2,95,1024]{2,0,1:T(2,128)}, u32[]{:S(2)}, u32[]{:S(2)}) collective-permute-start(f32[2,95,1024]{2,0,1:T(2,128)} %copy.70), channel_id=1, source_target_pairs={{0,4},{4,8},{8,12},{1,5},{5,9},{9,13},{2,6},{6,10},{10,14},{3,7},{... | collective-permute-start | bytes 2334728 | tf_op jit(solution)/shard_map/ppermute | solution.py:32
  585.1 2.3 add_select_fusion.6
  606.4 2.3 add_select_fusion
  632.0 2.4 fusion.12
  634.4 2.3 dynamic_update_slice.13
  636.8 2.4 fusion.11
  641.5 2.4 fusion.10
  647.8 10.6 %reduce-scatter.2.cloned.1.call-done = f32[2,160,1024]{2,1,0:T(8,128)} async-done(((f32[2,320,1024]{2,1,0:T(8,128)}), f32[2,160,1024]{2,1,0:T(8,128)}) %reduce-scatter.2.cloned.1.call-update) | async-done | bytes 1310736 | tf_op jit(solution)/shard_map/reduce_scatter | solution.py:119
  (156 shorter events, 113.9 us)
Async XLA Ops:
  6.5 12.0 %copy-start.26 = (s32[1,4]{1,0:T(1,128)S(1)}, s32[1,4]{1,0:T(1,128)}, u32[]{:S(2)}) copy-start(s32[1,4]{1,0:T(1,128)} %param.69) | copy-start | bytes 52
  6.5 651.8 %reduce-scatter.2.cloned.1.call-start = ((), (), s32[]{:S(2)}) async-start(), calls=%async_computation.1 | async-start | bytes 3932160 | tf_op jit(solution)/shard_map/reduce_scatter | solution.py:119
  9.8 2.0 copy-start.3
  12.2 11.7 %collective-permute-start = (f32[16,64,32]{1,2,0:T(8,128)S(1)}, f32[16,64,32]{1,2,0:T(8,128)S(1)}, u32[]{:S(2)}, u32[]{:S(2)}) collective-permute-start(f32[16,64,32]{1,2,0:T(8,128)S(1)} %copy.50), channel_id=1, source_target_pairs={{0,2},{1,3},{4,6},{5,7},{8,10},{9,11},{12,14},{13,15},{16,18},{17,... | collective-permute-start | bytes 393224 | tf_op jit(solution)/shard_map/ppermute | solution.py:23
  17.2 9.7 %collective-permute-start.1 = (f32[16,64,32]{1,2,0:T(8,128)S(1)}, f32[16,64,32]{1,2,0:T(8,128)S(1)}, u32[]{:S(2)}, u32[]{:S(2)}) collective-permute-start(f32[16,64,32]{1,2,0:T(8,128)S(1)} %copy.51), channel_id=1, source_target_pairs={{2,0},{3,1},{6,4},{7,5},{10,8},{11,9},{14,12},{15,13},{18,16},{19,... | collective-permute-start | bytes 393224 | tf_op jit(solution)/shard_map/ppermute | solution.py:24
  182.2 5.2 copy-start
  182.3 5.9 copy-start.1
  196.2 114.2 %collective-permute-start.2 = (bf16[2,16,32,1024]{3,2,1,0:T(8,128)(2,1)}, bf16[2,16,32,1024]{3,2,1,0:T(8,128)(2,1)}, u32[]{:S(2)}, u32[]{:S(2)}) collective-permute-start(bf16[2,16,32,1024]{3,2,1,0:T(8,128)(2,1)} %fusion.9), channel_id=1, source_target_pairs={{4,0},{8,4},{12,8},{5,1},{9,5},{13,9},{6,2},{10,6},{14,10},{7,3},{... | collective-permute-start | bytes 6291464 | tf_op jit(solution)/shard_map/ppermute | solution.py:32
  197.5 185.3 %collective-permute-start.4 = (bf16[2,16,32,1024]{3,2,1,0:T(8,128)(2,1)}, bf16[2,16,32,1024]{3,2,1,0:T(8,128)(2,1)}, u32[]{:S(2)}, u32[]{:S(2)}) collective-permute-start(bf16[2,16,32,1024]{3,2,1,0:T(8,128)(2,1)} %fusion.9), channel_id=1, source_target_pairs={{8,0},{12,4},{9,1},{13,5},{10,2},{14,6},{11,3},{15,7},{24,16},{28,... | collective-permute-start | bytes 6291464 | tf_op jit(solution)/shard_map/ppermute | solution.py:32
  198.8 257.0 %collective-permute-start.6 = (bf16[2,16,32,1024]{3,2,1,0:T(8,128)(2,1)}, bf16[2,16,32,1024]{3,2,1,0:T(8,128)(2,1)}, u32[]{:S(2)}, u32[]{:S(2)}) collective-permute-start(bf16[2,16,32,1024]{3,2,1,0:T(8,128)(2,1)} %fusion.9), channel_id=1, source_target_pairs={{12,0},{13,1},{14,2},{15,3},{28,16},{29,17},{30,18},{31,19}} | collective-permute-start | bytes 6291464 | tf_op jit(solution)/shard_map/ppermute | solution.py:32
  302.1 10.1 %copy-start.10 = (f32[1024,4,47]{0,2,1:T(8,128)}, f32[1024,4,47]{0,2,1:T(8,128)S(1)}, u32[]{:S(2)}) copy-start(f32[1024,4,47]{0,2,1:T(8,128)S(1)} %fusion.31) | copy-start | bytes 2310148
  305.9 6.3 copy-start.19
  309.0 3.2 copy-start.21
  352.1 0.9 copy-start.17
  352.9 0.7 copy-start.22
  381.3 0.9 copy-start.13
  382.2 0.7 copy-start.24
  424.5 29.9 %copy-start.14 = (f32[1024,4,47]{0,2,1:T(8,128)}, f32[1024,4,47]{0,2,1:T(8,128)S(1)}, u32[]{:S(2)}) copy-start(f32[1024,4,47]{0,2,1:T(8,128)S(1)} %fusion.21) | copy-start | bytes 2310148
  448.5 3.5 copy-start.23
  448.6 3.5 copy-start.25
  451.9 2.5 copy-start.11
  508.8 0.9 copy-start.18
  521.8 6.6 copy-start.5
  525.1 0.9 copy-start.15
  536.4 56.2 %copy-start.6 = (f32[1024,95]{0,1:T(8,128)}, f32[1024,95]{0,1:T(8,128)S(1)}, u32[]{:S(2)}) copy-start(f32[1024,95]{0,1:T(8,128)S(1)} %scatter-add.131) | copy-start | bytes 1167364
  536.5 54.8 %copy-start.12 = (f32[1024,4,47]{0,2,1:T(8,128)S(1)}, f32[1024,4,47]{0,2,1:T(8,128)}, u32[]{:S(2)}) copy-start(f32[1024,4,47]{0,2,1:T(8,128)} %copy-done.11) | copy-start | bytes 2310148
  548.4 83.6 %collective-permute-start.3 = (f32[2,95,1024]{2,0,1:T(2,128)}, f32[2,95,1024]{2,0,1:T(2,128)}, u32[]{:S(2)}, u32[]{:S(2)}) collective-permute-start(f32[2,95,1024]{2,0,1:T(2,128)} %copy.70), channel_id=1, source_target_pairs={{0,4},{4,8},{8,12},{1,5},{5,9},{9,13},{2,6},{6,10},{10,14},{3,7},{... | collective-permute-start | bytes 2334728 | tf_op jit(solution)/shard_map/ppermute | solution.py:32
  589.4 22.4 %copy-start.4 = (f32[1024,95]{0,1:T(8,128)}, f32[1024,95]{0,1:T(8,128)S(1)}, u32[]{:S(2)}) copy-start(f32[1024,95]{0,1:T(8,128)S(1)} %scatter-add.145) | copy-start | bytes 1167364
  595.2 15.3 %copy-start.16 = (f32[1024,4,47]{0,2,1:T(8,128)S(1)}, f32[1024,4,47]{0,2,1:T(8,128)}, u32[]{:S(2)}) copy-start(f32[1024,4,47]{0,2,1:T(8,128)} %copy-done.15) | copy-start | bytes 2310148
  598.3 38.5 %collective-permute-start.5 = (f32[2,95,1024]{2,0,1:T(2,128)}, f32[2,95,1024]{2,0,1:T(2,128)}, u32[]{:S(2)}, u32[]{:S(2)}) collective-permute-start(f32[2,95,1024]{2,0,1:T(2,128)} %copy.80), channel_id=1, source_target_pairs={{0,8},{4,12},{1,9},{5,13},{2,10},{6,14},{3,11},{7,15},{16,24},{20,... | collective-permute-start | bytes 2334728 | tf_op jit(solution)/shard_map/ppermute | solution.py:32
  600.5 23.1 %copy-start.20 = (f32[1024,95]{0,1:T(8,128)S(1)}, f32[1024,95]{0,1:T(8,128)}, u32[]{:S(2)}) copy-start(f32[1024,95]{0,1:T(8,128)} %copy-done.19) | copy-start | bytes 1167364
  616.5 10.9 %copy-start.7 = (f32[1024,95]{0,1:T(8,128)}, f32[1024,95]{0,1:T(8,128)S(1)}, u32[]{:S(2)}) copy-start(f32[1024,95]{0,1:T(8,128)S(1)} %scatter-add.159) | copy-start | bytes 1167364
  618.0 9.3 %copy-start.9 = (f32[1024,95]{0,1:T(8,128)}, f32[1024,95]{0,1:T(8,128)S(1)}, u32[]{:S(2)}) copy-start(f32[1024,95]{0,1:T(8,128)S(1)} %scatter-add.151) | copy-start | bytes 1167364
  619.6 21.9 %collective-permute-start.7 = (f32[2,95,1024]{2,0,1:T(2,128)}, f32[2,95,1024]{2,0,1:T(2,128)}, u32[]{:S(2)}, u32[]{:S(2)}) collective-permute-start(f32[2,95,1024]{2,0,1:T(2,128)} %copy.90), channel_id=1, source_target_pairs={{0,12},{1,13},{2,14},{3,15},{16,28},{17,29},{18,30},{19,31}} | collective-permute-start | bytes 2334728 | tf_op jit(solution)/shard_map/ppermute | solution.py:32
  634.4 7.1 %copy-start.8 = (f32[1024,95]{0,1:T(8,128)S(1)}, f32[1024,95]{0,1:T(8,128)}, u32[]{:S(2)}) copy-start(f32[1024,95]{0,1:T(8,128)} %copy-done.7) | copy-start | bytes 1167364
  646.3 1.5 copy-start.2
Sparse Core Ops, SparseCore 0:
  647.9 10.4 reduce-scatter.1
where the time goes:
time: 678 us; the launch traced here: 665 us
  local copies, waits for them, and re-layouts  257 us (38%)
  other arithmetic  215 us (32%)
  matrix products  118 us (17%)
  starting transfers between devices  45.2 us (7%)
  between operations  17.1 us (3%)
  waiting for transfers between devices  13.4 us (2%)
    another operation x1, other arithmetic, whiten_rows(): lax.reduce_window(padded, jnp.zeros((), padded.dtype), lax.add, (1, 1, wi...  149 us
    concatenate x4, local copies, waits for them, and re-layouts, correlate(): right_both = jnp.concatenate([right_rows[0], right_rows[1]], axis=0)  54.1 us
    convert_element_type x4, local copies, waits for them, and re-layouts, correlate(): corr_real = (jnp.einsum('wif,wjf->fij', left_real, right_both, preferred_...  48.9 us
    convert_element_type x4, local copies, waits for them, and re-layouts, correlate(): corr_imag = (jnp.einsum('wif,wjf->fij', left_imag, right_both, preferred_...  48.2 us
    dot_general x4, matrix products, correlate(): jnp.einsum('wif,wjf->fij', left_real, right_both, preferred_element_type=...  45.6 us
    dot_general x4, matrix products, correlate(): jnp.einsum('wif,wjf->fij', left_imag, right_both, preferred_element_type=...  45.4 us
    scatter-add x32, local copies, waits for them, and re-layouts, lag_stack(): lag_sums.at[:, first_lag:first_lag + col_count + band_rows - 1]  41.9 us
    ppermute x6, starting transfers between devices, from_behind(): return lax.ppermute(block, axis, route)  39 us
  transfers between devices with their start and end apart: 9, of which 2 were waited for; matrix products, arithmetic and copies ran while one was open for 47% of the time, Pallas kernels for 0%

commit v1 on v0

--- a/solution.py
+++ b/solution.py
@@ -2,7 +2,10 @@
 
 import jax
 import jax.numpy as jnp
+import numpy as np
 from jax import lax
+from jax.experimental import pallas as pl
+from jax.experimental.pallas import tpu as pltpu
 from jax.sharding import PartitionSpec as P
 
 REACH = 3
@@ -87,7 +90,7 @@
     return jnp.stack([lag_stack(corr_real, lag_table), lag_stack(corr_imag, lag_table)])
 
 
-def shards(spectra, counts, owners):
+def general_shards(spectra, counts, owners):
     pair_devs = lax.axis_size("pairs")
     member = lax.axis_index("pairs")
     channels = spectra.shape[2]
@@ -120,7 +123,345 @@
     return summed[:, None]
 
 
+EDGE = 128
+BAND = 128
+GROUP = 4
+F32 = jnp.float32
+MESH = pl.DeviceIdType.MESH
+
+
+def channel_transforms(channels, factor):
+    points = 2 * channels
+    index = np.arange(points)
+    angle = 2 * np.pi * np.outer(index, np.arange(channels)) / points
+    cos, sin = np.cos(angle), np.sin(angle)
+    full = np.block([[cos, sin], [-sin, cos]])
+    high = full.astype(jnp.bfloat16)
+    low = (full - high.astype(np.float64)).astype(jnp.bfloat16)
+    forward = np.concatenate([high, low], axis=1)
+    angle = 2 * np.pi * np.outer(index - (channels - 1), index) / points
+    cos, sin = np.cos(angle), np.sin(angle)
+    cos[-1], sin[-1] = 0.0, 0.0
+    inverse = np.block([[cos, sin], [-sin, cos]]) * (factor / points)
+    return jnp.asarray(forward), jnp.asarray(inverse.astype(np.float32))
+
+
+def stack_kernel(
+    x_ref, flag_ref, forward_ref, inverse_ref, out_ref,
+    white, far, back, spec, other, sums, sums_back, stack, piece_out, piece_back, piece_in, arrived, swapped, seen,
+    chain_send, chain_recv, back_send, back_recv, piece_send, piece_recv,
+    next_send, next_recv, swap_send, swap_recv, flag_send, flag_recv,
+):
+    windows, channels, length = x_ref.shape[1:]
+    half = length - 2 * EDGE
+    bands, groups = half // BAND, windows // GROUP
+    points = 2 * channels
+    kept = out_ref.shape[1]
+    blocks, halves = lax.axis_size("cable"), lax.axis_size("pairs")
+    z, m = lax.axis_index("cable"), lax.axis_index("pairs")
+    onward = {"cable": lax.rem(z + 1, blocks)}
+    backward = {"cable": lax.rem(z + blocks - 1, blocks)}
+    partner = {"pairs": lax.rem(m + 1, halves)}
+
+    def remote(source, target, send, recv, device):
+        return pltpu.make_async_remote_copy(
+            src_ref=source, dst_ref=target, send_sem=send, recv_sem=recv, device_id=device, device_id_type=MESH
+        )
+
+    def first_hop(s):
+        return remote(white.at[s], far.at[s], chain_send.at[s], chain_recv.at[s], onward)
+
+    def next_hop(s):
+        return remote(far.at[s], far.at[s], chain_send.at[s], chain_recv.at[s], onward)
+
+    def back_hop(s):
+        return remote(white.at[s], back.at[s], back_send.at[s], back_recv.at[s], backward)
+
+    def to_first(c, slot):
+        return remote(piece_out.at[c], piece_in.at[slot, c], piece_send.at[c], piece_recv.at[slot, c], {"cable": 0})
+
+    def to_next(c):
+        return remote(piece_back.at[c], arrived.at[c], next_send.at[c], next_recv.at[c], onward)
+
+    def swap(c):
+        rows = pl.ds(pl.multiple_of((1 - m) * kept, 8), kept)
+        return remote(stack.at[c, :, rows], swapped.at[c], swap_send.at[c], swap_recv.at[c], partner)
+
+    def flags_to(block):
+        return remote(flag_ref, seen, flag_send.at[block - 1], flag_recv.at[0], {"cable": block})
+
+    barrier = pltpu.get_barrier_semaphore()
+    for step in range(1, blocks):
+        pl.semaphore_signal(barrier, inc=1, device_id={"cable": lax.rem(z + step, blocks)}, device_id_type=MESH)
+    pl.semaphore_signal(barrier, inc=1, device_id=partner, device_id_type=MESH)
+    pl.semaphore_wait(barrier, blocks)
+
+    @pl.when(z == 0)
+    def _():
+        for block in range(1, blocks):
+            flags_to(block).start()
+
+    def whiten(q, carry):
+        for i in range(GROUP):
+            real = x_ref[0, q * GROUP + i].astype(F32)
+            imag = x_ref[1, q * GROUP + i].astype(F32)
+            power = real * real + imag * imag
+            total, width = power, 1
+            while width < 2 * HALF_WIDTH:
+                total = total + pltpu.roll(total, width, 1)
+                width *= 2
+            total = total + pltpu.roll(power, width, 1)
+            total = pltpu.roll(total, length - HALF_WIDTH, 1)[:, EDGE : EDGE + half]
+            gain = lax.rsqrt(total / (2 * HALF_WIDTH + 1) + epsilon)
+            real = (real[:, EDGE : EDGE + half] * gain).astype(jnp.bfloat16)
+            imag = (imag[:, EDGE : EDGE + half] * gain).astype(jnp.bfloat16)
+            for c in range(bands):
+                white[c * groups + q, i, :channels] = real[:, c * BAND : (c + 1) * BAND]
+                white[c * groups + q, i, channels:] = imag[:, c * BAND : (c + 1) * BAND]
+
+        @pl.when(z == 0)
+        def _():
+            first_hop(q).start()
+
+        @pl.when(z == blocks - 1)
+        def _():
+            back_hop(q).start()
+
+        return carry
+
+    lax.fori_loop(0, groups, whiten, 0)
+
+    @pl.when(z == 0)
+    def _():
+        @pl.loop(groups, bands * groups)
+        def _(s):
+            first_hop(s).start()
+
+    @pl.when(z == blocks - 1)
+    def _():
+        @pl.loop(groups, bands * groups)
+        def _(s):
+            back_hop(s).start()
+
+    def transform(buffer, s):
+        wide = jnp.concatenate([buffer[s, i] for i in range(GROUP)], axis=1)
+        return jnp.dot(forward_ref[...], jnp.concatenate([wide, wide], axis=0), preferred_element_type=F32)
+
+    tile = 32
+
+    def power_into(total, s):
+        for k in range(0, points, tile):
+            gained = total[k : k + tile]
+            for i in range(GROUP):
+                lanes = slice(i * BAND, (i + 1) * BAND)
+                real = spec[s, k : k + tile, lanes]
+                imag = spec[s, points + k : points + k + tile, lanes]
+                gained = gained + (real * real + imag * imag)
+            total[k : k + tile] = gained
+
+    def cross_into(total, s, sign):
+        for k in range(0, points, tile):
+            gained_real = total[k : k + tile]
+            gained_imag = total[points + k : points + k + tile]
+            for i in range(GROUP):
+                lanes = slice(i * BAND, (i + 1) * BAND)
+                own_real = spec[s, k : k + tile, lanes]
+                own_imag = spec[s, points + k : points + k + tile, lanes]
+                real = other[k : k + tile, lanes]
+                imag = other[points + k : points + k + tile, lanes]
+                gained_real = gained_real + (own_real * real + own_imag * imag)
+                if sign > 0:
+                    gained_imag = gained_imag + (own_imag * real - own_real * imag)
+                else:
+                    gained_imag = gained_imag + (own_real * imag - own_imag * real)
+            total[k : k + tile] = gained_real
+            total[points + k : points + k + tile] = gained_imag
+
+    def lags_of(values, columns):
+        return jnp.dot(
+            inverse_ref[:, :columns], values, preferred_element_type=F32, precision=lax.Precision.HIGHEST
+        )
+
+    def add_piece(c, first, piece):
+        rows = pl.ds(first, points)
+        stack[c, 0, rows] += piece[:points]
+        stack[c, 1, rows] += piece[points:]
+
+    def own_band(c, carry):
+        sums[...] = jnp.zeros_like(sums)
+
+        def step(q, inner):
+            s = c * groups + q
+            spec[s] = transform(white, s)
+            power_into(sums, s)
+            return inner
+
+        lax.fori_loop(0, groups, step, 0)
+        stack[c] = jnp.zeros(stack.shape[1:], F32)
+        add_piece(c, 0, flag_ref[REACH + 1 : REACH + 2, :] * lags_of(sums[:points], points))
+        return carry
+
+    lax.fori_loop(0, bands, own_band, 0)
+
+    @pl.when(z > 0)
+    def _():
+        flags_to(1).wait_recv()
+
+        def far_band(c, carry):
+            sums[...] = jnp.zeros_like(sums)
+            sums_back[...] = jnp.zeros_like(sums_back)
+
+            def step(q, inner):
+                s = c * groups + q
+                next_hop(s).wait_recv()
+
+                @pl.when(z < blocks - 1)
+                def _():
+                    next_hop(s).start()
+
+                other[...] = transform(far, s)
+                cross_into(sums, s, -1)
+
+                @pl.when(z == blocks - 2)
+                def _():
+                    back_hop(s).wait_recv()
+                    other[...] = transform(back, s)
+                    cross_into(sums_back, s, 1)
+
+                return inner
+
+            lax.fori_loop(0, groups, step, 0)
+            piece = lags_of(sums[...], 2 * points)
+            piece_out[c] = piece
+            to_first(c, z - 1).start()
+            counted = seen[pl.ds(z, 1), :] * seen[pl.ds(REACH + 1 + z, 1), :]
+            add_piece(c, pl.multiple_of(z * channels, 8), counted * piece)
+
+            @pl.when(z == blocks - 2)
+            def _():
+                piece = flag_ref[REACH + 2 : REACH + 3, :] * lags_of(sums_back[...], 2 * points)
+                sent = flag_ref[1:2, :]
+                piece_back[c] = sent * piece
+                to_next(c).start()
+                add_piece(c, channels, (1.0 - sent) * piece)
+
+            @pl.when(z == blocks - 1)
+            def _():
+                to_next(c).wait_recv()
+                add_piece(c, channels, arrived[c])
+
+            swap(c).start()
+            return carry
+
+        lax.fori_loop(0, bands, far_band, 0)
+
+    @pl.when(z == 0)
+    def _():
+        def near_band(c, carry):
+            for offset in range(1, blocks):
+                to_first(c, offset - 1).wait_recv()
+                counted = (1.0 - flag_ref[offset : offset + 1, :]) * flag_ref[REACH + 1 + offset : REACH + 2 + offset, :]
+                add_piece(c, offset * channels, counted * piece_in[offset - 1, c])
+            swap(c).start()
+            return carry
+
+        lax.fori_loop(0, bands, near_band, 0)
+
+    def collect(c, carry):
+        mine = pl.ds(pl.multiple_of(m * half + c * BAND, BAND), BAND)
+        theirs = pl.ds(pl.multiple_of((1 - m) * half + c * BAND, BAND), BAND)
+        out_ref[:, :, mine] = stack[c, :, pl.ds(pl.multiple_of(m * kept, 8), kept)]
+        swap(c).wait_recv()
+        out_ref[:, :, theirs] = swapped[c]
+        swap(c).wait_send()
+        return carry
+
+    lax.fori_loop(0, bands, collect, 0)
+
+    @pl.when(z < blocks - 1)
+    def _():
+        @pl.loop(0, bands * groups)
+        def _(s):
+            next_hop(s).wait_send()
+
+    @pl.when(z == blocks - 1)
+    def _():
+        @pl.loop(0, bands * groups)
+        def _(s):
+            back_hop(s).wait_send()
+
+    @pl.when(z > 0)
+    def _():
+        @pl.loop(0, bands)
+        def _(c):
+            to_first(c, z - 1).wait_send()
+
+    @pl.when(z == blocks - 2)
+    def _():
+        @pl.loop(0, bands)
+        def _(c):
+            to_next(c).wait_send()
+
+    @pl.when(z == 0)
+    def _():
+        for block in range(1, blocks):
+            flags_to(block).wait_send()
+
+
+def four_block_shards(spectra, counts, owners):
+    parts, windows, channels, bins = spectra.shape
+    halves, member = lax.axis_size("pairs"), lax.axis_index("pairs")
+    blocks, z = lax.axis_size("cable"), lax.axis_index("cable")
+    half, points = bins // halves, 2 * channels
+    pad = jnp.zeros((parts, windows, channels, EDGE - HALF_WIDTH), spectra.dtype)
+    padded = with_halo(spectra, (("bins", 3),), HALF_WIDTH)
+    padded = jnp.concatenate([pad, padded, pad], axis=3)
+    padded = lax.dynamic_slice_in_dim(padded, member * half, half + 2 * EDGE, 3)
+    live = jnp.minimum(counts[0], blocks - z)
+    weights = (jnp.arange(REACH + 1) < live).astype(F32)
+    flags = jnp.concatenate([owners[0].astype(F32), weights])
+    flags = jnp.broadcast_to(flags[:, None], (2 * (REACH + 1), BAND))
+    forward, inverse = channel_transforms(channels, 1.0 / math.sqrt(windows * channels))
+    bands, groups = half // BAND, windows // GROUP
+    pieces = bands * groups
+    rows = (REACH + 2) * channels
+    kept = rows // halves
+    block = pltpu.VMEM((pieces, GROUP, points, BAND), jnp.bfloat16)
+    lags = pltpu.VMEM((bands, 2 * points, BAND), F32)
+    dma = pltpu.SemaphoreType.DMA
+    out = pl.pallas_call(
+        stack_kernel,
+        out_shape=jax.ShapeDtypeStruct((2, kept, bins), F32),
+        in_specs=[pl.BlockSpec(memory_space=pltpu.VMEM)] * 4,
+        out_specs=pl.BlockSpec(memory_space=pltpu.VMEM),
+        scratch_shapes=[
+            block, block, block,
+            pltpu.VMEM((pieces, 2 * points, GROUP * BAND), F32),
+            pltpu.VMEM((2 * points, GROUP * BAND), F32),
+            pltpu.VMEM((2 * points, BAND), F32),
+            pltpu.VMEM((2 * points, BAND), F32),
+            pltpu.VMEM((bands, 2, rows, BAND), F32),
+            lags, lags,
+            pltpu.VMEM((blocks - 1, bands, 2 * points, BAND), F32),
+            lags,
+            pltpu.VMEM((bands, 2, kept, BAND), F32),
+            pltpu.VMEM(flags.shape, F32),
+            dma((pieces,)), dma((pieces,)), dma((pieces,)), dma((pieces,)),
+            dma((bands,)), dma((blocks - 1, bands)),
+            dma((bands,)), dma((bands,)), dma((bands,)), dma((bands,)),
+            dma((blocks - 1,)), dma((1,)),
+        ],
+        compiler_params=pltpu.CompilerParams(
+            collective_id=0, has_side_effects=True, vmem_limit_bytes=60 * 1024 * 1024
+        ),
+    )(padded, flags, forward, inverse)
+    return out[:, None]
+
+
 def solution(mesh):
+    sizes = dict(mesh.shape)
+    fits = sizes["cable"] == REACH + 1 and sizes["pairs"] == 2
+    shards = four_block_shards if fits else general_shards
     placed = (
         P("groups", None, "cable", "bins"),
         P(("groups", "cable")),

time: 678 us -> 129 us (0.19); the launches traced: 665 us -> 128 us
  local copies, waits for them, and re-layouts: 257 us -> 17.7 us
  other arithmetic: 215 us -> 0.74 us
  matrix products: 118 us -> 0 us
  Pallas kernels: 0 us -> 90.1 us
  starting transfers between devices: 45.2 us -> 6.2 us
  between operations: 17.1 us -> 0.7 us
    another operation x25 -> x0, other arithmetic: 185 us -> none  [the longest x1 149 us: whiten_rows(): lax.reduce_window(padded, jnp.zeros((), padded.dtype), lax.add, (1, 1, wi...]
    dot_general x16 -> x0, matrix products: 118 us -> none  [the longest x4 45.6 us: correlate(): jnp.einsum('wif,wjf->fij', left_real, right_both, preferred_element_type=...]
    convert_element_type x8 -> x0, local copies, waits for them, and re-layouts: 97.1 us -> none  [the longest x4 48.9 us: correlate(): corr_real = (jnp.einsum('wif,wjf->fij', left_real, right_both, preferred_...]
    pallas_call x0 -> x1, Pallas kernels: none -> 90.1 us  [four_block_shards(): pl.pallas_call(stack_kernel, out_shape=jax.ShapeDtypeStruct((2, kept, bin...]
    concatenate x7 -> x1, local copies, waits for them, and re-layouts: 86.4 us -> 9.11 us  [four_block_shards(): padded = jnp.concatenate([pad, padded, pad], axis=3)]
    scatter-add x32 -> x0, local copies, waits for them, and re-layouts: 41.9 us -> none  [lag_stack(): lag_sums.at[:, first_lag:first_lag + col_count + band_rows - 1]]
    ppermute x6 -> x0, starting transfers between devices: 39 us -> none  [from_behind(): return lax.ppermute(block, axis, route)]
    reduce_scatter x1 -> x0, waiting for transfers between devices: 10.6 us -> none  [shards(): summed = lax.psum_scatter(stacks, 'pairs', scatter_dimension=1, tiled=True)]
  transfers between devices with their start and end apart: 9 -> 2, of which waited for: 2 -> 2; matrix products, arithmetic and copies ran while one was open for 47% -> 1% of each run, Pallas kernels for 0% -> 0%
where the time goes in v1:
time: 129 us; the launch traced here: 128 us
  Pallas kernels  90.1 us (70%)
  local copies, waits for them, and re-layouts  17.7 us (14%)
  waiting for transfers between devices  12.6 us (10%)
  starting transfers between devices  6.2 us (5%)
    pallas_call x1, Pallas kernels, four_block_shards(): pl.pallas_call(stack_kernel, out_shape=jax.ShapeDtypeStruct((2, kept, bin...  90.1 us
    concatenate x1, local copies, waits for them, and re-layouts, four_block_shards(): padded = jnp.concatenate([pad, padded, pad], axis=3)  9.11 us
    ppermute x1, waiting for transfers between devices, with_halo(): before = lax.ppermute(last, axis, up)  8.44 us
    ppermute x1, starting transfers between devices, with_halo(): before = lax.ppermute(last, axis, up)  4.9 us
    ppermute x1, waiting for transfers between devices, with_halo(): after = lax.ppermute(first, axis, down)  4.15 us
    dynamic_slice x1, local copies, waits for them, and re-layouts, four_block_shards(): padded = lax.dynamic_slice_in_dim(padded, member * half, half + 2 * EDGE, 3)  3.88 us
  transfers between devices with their start and end apart: 2, of which 2 were waited for; matrix products, arithmetic and copies ran while one was open for 1% of the time, Pallas kernels for 0%

profile of v1, /device:TPU:0, one launch (start us, length us, event | category | flops | bytes accessed | tf_op | source)
XLA Modules:
  0.0 128.1 jit_solution(7597018134055572668)
XLA Ops:
  0.0 1.5 %fusion = (bf16[2,16,64,32]{3,2,1,0:T(8,128)(2,1)S(1)}, bf16[2,16,64,32]{3,2,1,0:T(8,128)(2,1)S(1)}) fusion(bf16[2,16,64,1024]{3,2,1,0:T(8,128)(2,1)} %param.5), kind=kLoop, calls=%fused_computation.4 | loop fusion | bytes 524288 | tf_op jit(solution)/shard_map/slice | solution.py:25
  1.5 4.9 %collective-permute-start = (bf16[2,16,64,32]{3,2,1,0:T(8,128)(2,1)S(1)}, bf16[2,16,64,32]{3,2,1,0:T(8,128)(2,1)S(1)}, u32[]{:S(2)}, u32[]{:S(2)}) collective-permute-start(bf16[2,16,64,32]{3,2,1,0:T(8,128)(2,1)S(1)} %get-tuple-element.6), channel_id=1, source_target_pairs={{0,2},{1,3},{4,6},{5,7},{8,10},{9,11},{12,14},{13,15},{16,18},{17,... | collective-permute-start | bytes 393224 | tf_op jit(solution)/shard_map/ppermute | solution.py:26
  6.4 1.3 %collective-permute-start.1 = (bf16[2,16,64,32]{3,2,1,0:T(8,128)(2,1)S(1)}, bf16[2,16,64,32]{3,2,1,0:T(8,128)(2,1)S(1)}, u32[]{:S(2)}, u32[]{:S(2)}) collective-permute-start(bf16[2,16,64,32]{3,2,1,0:T(8,128)(2,1)S(1)} %get-tuple-element.5), channel_id=1, source_target_pairs={{2,0},{3,1},{6,4},{7,5},{10,8},{11,9},{14,12},{15,13},{18,16},{19,... | collective-permute-start | bytes 393224 | tf_op jit(solution)/shard_map/ppermute | solution.py:27
  8.3 0.7 convert_bitcast_fusion
  9.0 0.1 pad_maximum_fusion
  9.1 8.4 %collective-permute-done = bf16[2,16,64,32]{3,2,1,0:T(8,128)(2,1)S(1)} collective-permute-done((bf16[2,16,64,32]{3,2,1,0:T(8,128)(2,1)S(1)}, bf16[2,16,64,32]{3,2,1,0:T(8,128)(2,1)S(1)}, u32[]{:S(2)}, u32[]{:S(2)}) %collective-permute-start) | collective-permute-done | bytes 131104 | tf_op jit(solution)/shard_map/ppermute | solution.py:26
  17.5 4.1 %collective-permute-done.1 = bf16[2,16,64,32]{3,2,1,0:T(8,128)(2,1)S(1)} collective-permute-done((bf16[2,16,64,32]{3,2,1,0:T(8,128)(2,1)S(1)}, bf16[2,16,64,32]{3,2,1,0:T(8,128)(2,1)S(1)}, u32[]{:S(2)}, u32[]{:S(2)}) %collective-permute-start.1) | collective-permute-done | bytes 131104 | tf_op jit(solution)/shard_map/ppermute | solution.py:27
  21.7 0.1 broadcast_in_dim.12
  21.8 9.1 %concatenate.6 = bf16[2,16,64,1280]{3,2,1,0:T(8,128)(2,1)} concatenate(bf16[2,16,64,96]{3,2,1,0:T(8,128)(2,1)S(1)} %broadcast_in_dim.12, bf16[2,16,64,32]{3,2,1,0:T(8,128)(2,1)S(1)} %collective-permute-done, bf16[2,16,64,1024]{3,2,1,0:T(8,128)(2,1)} %param.5, bf16[2,16,64,32]{3,2,1,0:T(8,128)(2,1)S(1)} %collective-permute-done.1, bf16[2,16,64,96]{3,2,1,0:T(8,128)(2,1)S(1)} %broadcast_in_dim.12), dimensions={3} | concatenate | bytes 10485760 | tf_op jit(solution)/shard_map/concatenate | solution.py:418
  30.9 3.9 %constant_dynamic-slice_fusion.x_ref = bf16[2,16,64,768]{3,2,1,0:T(8,128)(2,1)} fusion(bf16[2,16,64,1280]{3,2,1,0:T(8,128)(2,1)} %concatenate.6, s32[]{:T(128)S(6)} %select_n.3), kind=kLoop, calls=%fused_computation.3 | loop fusion | bytes 6291460 | tf_op jit(solution)/shard_map/dynamic_slice | solution.py:419
  34.8 0.7 broadcast_in_dim.13.flag_ref
  35.4 90.1 %shard_map.55 = f32[2,160,1024]{2,1,0:T(8,128)} custom-call(bf16[2,16,64,768]{3,2,1,0:T(8,128)(2,1)} %constant_dynamic-slice_fusion.x_ref, f32[8,128]{1,0:T(8,128)} %broadcast_in_dim.13.flag_ref, bf16[256,256]{1,0:T(8,128)(2,1)} %constant.23.clone.forward_ref, f32[256,256]{1,0:T(8,128)} %constant.24.clone.inverse_ref), custom_call_target="tpu_custom_call" | custom-call | tf_op jit(solution)/shard_map/pallas_call | solution.py:432
  125.6 2.5 %copy.9 = f32[2,1,160,1024]{3,2,1,0:T(8,128)} copy(f32[2,1,160,1024]{3,2,1,0:T(8,128)} %bitcast.7) | data formatting | bytes 2621440
  (1 shorter events, 0.0 us)
Async XLA Ops:
  1.5 16.0 %collective-permute-start = (bf16[2,16,64,32]{3,2,1,0:T(8,128)(2,1)S(1)}, bf16[2,16,64,32]{3,2,1,0:T(8,128)(2,1)S(1)}, u32[]{:S(2)}, u32[]{:S(2)}) collective-permute-start(bf16[2,16,64,32]{3,2,1,0:T(8,128)(2,1)S(1)} %get-tuple-element.6), channel_id=1, source_target_pairs={{0,2},{1,3},{4,6},{5,7},{8,10},{9,11},{12,14},{13,15},{16,18},{17,... | collective-permute-start | bytes 393224 | tf_op jit(solution)/shard_map/ppermute | solution.py:26
  6.4 15.3 %collective-permute-start.1 = (bf16[2,16,64,32]{3,2,1,0:T(8,128)(2,1)S(1)}, bf16[2,16,64,32]{3,2,1,0:T(8,128)(2,1)S(1)}, u32[]{:S(2)}, u32[]{:S(2)}) collective-permute-start(bf16[2,16,64,32]{3,2,1,0:T(8,128)(2,1)S(1)} %get-tuple-element.5), channel_id=1, source_target_pairs={{2,0},{3,1},{6,4},{7,5},{10,8},{11,9},{14,12},{15,13},{18,16},{19,... | collective-permute-start | bytes 393224 | tf_op jit(solution)/shard_map/ppermute | solution.py:27

commit v2 on v1

--- a/solution.py
+++ b/solution.py
@@ -147,18 +147,22 @@
 
 
 def stack_kernel(
-    x_ref, flag_ref, forward_ref, inverse_ref, out_ref,
-    white, far, back, spec, other, sums, sums_back, stack, piece_out, piece_back, piece_in, arrived, swapped, seen,
+    spectra_ref, counts_ref, owners_ref, forward_ref, inverse_ref, out_ref,
+    x_ref, flag_ref, white, far, back, spec, other, sums, sums_back, stack, piece_out, piece_back, piece_in, arrived, swapped, seen,
     chain_send, chain_recv, back_send, back_recv, piece_send, piece_recv,
-    next_send, next_recv, swap_send, swap_recv, flag_send, flag_recv,
+    next_send, next_recv, swap_send, swap_recv, flag_send, flag_recv, load_sem, edge_send, edge_recv,
 ):
-    windows, channels, length = x_ref.shape[1:]
-    half = length - 2 * EDGE
+    windows, channels = x_ref.shape[1:3]
+    half = x_ref.shape[3] - 2 * EDGE
     bands, groups = half // BAND, windows // GROUP
     points = 2 * channels
     kept = out_ref.shape[1]
     blocks, halves = lax.axis_size("cable"), lax.axis_size("pairs")
     z, m = lax.axis_index("cable"), lax.axis_index("pairs")
+    cuts, x = lax.axis_size("bins"), lax.axis_index("bins")
+    bins = spectra_ref.shape[3]
+    first = m == 0
+    mirrored = jnp.where((x > 0) & (first | (x == cuts - 1)), 1, 0)
     onward = {"cable": lax.rem(z + 1, blocks)}
     backward = {"cable": lax.rem(z + blocks - 1, blocks)}
     partner = {"pairs": lax.rem(m + 1, halves)}
@@ -185,39 +189,90 @@
 
     def swap(c):
         rows = pl.ds(pl.multiple_of((1 - m) * kept, 8), kept)
-        return remote(stack.at[c, :, rows], swapped.at[c], swap_send.at[c], swap_recv.at[c], partner)
+        return remote(
+            stack.at[c, :, rows], swapped.at[place(c)], swap_send.at[c], swap_recv.at[place(c)], partner
+        )
+
+    def place(c):
+        return c + mirrored * (bands - 1 - 2 * c)
+
+    def load(q):
+        near = pl.multiple_of(m * (half - EDGE), EDGE)
+        spot = pl.multiple_of((1 - m) * EDGE, EDGE)
+        rows = pl.ds(q * GROUP, GROUP)
+        return pltpu.make_async_copy(
+            spectra_ref.at[:, rows, :, pl.ds(near, half + EDGE)],
+            x_ref.at[:, rows, :, pl.ds(spot, half + EDGE)],
+            load_sem.at[q],
+        )
+
+    spot = pl.ds(pl.multiple_of(m * (half + EDGE), EDGE), EDGE)
+
+    def edge():
+        source = pl.ds(pl.multiple_of((1 - m) * (bins - EDGE), EDGE), EDGE)
+        target = {"bins": lax.rem(x + cuts + 1 - 2 * m, cuts)}
+        return remote(
+            spectra_ref.at[:, :, :, source], x_ref.at[:, :, :, spot], edge_send.at[0], edge_recv.at[0], target
+        )
 
     def flags_to(block):
         return remote(flag_ref, seen, flag_send.at[block - 1], flag_recv.at[0], {"cable": block})
 
+    for q in range(groups):
+        load(q).start()
+    live = jnp.minimum(counts_ref[0], blocks - z)
+    for offset in range(REACH + 1):
+        flag_ref[offset : offset + 1, :] = jnp.full((1, BAND), owners_ref[0, offset].astype(F32))
+        weight = jnp.where(offset < live, 1.0, 0.0)
+        flag_ref[REACH + 1 + offset : REACH + 2 + offset, :] = jnp.full((1, BAND), weight)
     barrier = pltpu.get_barrier_semaphore()
     for step in range(1, blocks):
         pl.semaphore_signal(barrier, inc=1, device_id={"cable": lax.rem(z + step, blocks)}, device_id_type=MESH)
     pl.semaphore_signal(barrier, inc=1, device_id=partner, device_id_type=MESH)
-    pl.semaphore_wait(barrier, blocks)
+    for step in range(1, cuts):
+        pl.semaphore_signal(barrier, inc=1, device_id={"bins": lax.rem(x + step, cuts)}, device_id_type=MESH)
+    pl.semaphore_wait(barrier, blocks + cuts - 1)
+    sends_edge = (first & (x < cuts - 1)) | (~first & (x > 0))
+    takes_edge = (first & (x > 0)) | (~first & (x < cuts - 1))
+
+    @pl.when(sends_edge)
+    def _():
+        edge().start()
+
+    @pl.when(~takes_edge)
+    def _():
+        x_ref[:, :, :, spot] = jnp.zeros((2, windows, channels, EDGE), x_ref.dtype)
+
 
     @pl.when(z == 0)
     def _():
         for block in range(1, blocks):
             flags_to(block).start()
 
-    def whiten(q, carry):
+    def whiten(q, begin, count, store):
+        length = count * BAND + 2 * EDGE
+        lanes = pl.ds(pl.multiple_of(begin, BAND), length)
         for i in range(GROUP):
-            real = x_ref[0, q * GROUP + i].astype(F32)
-            imag = x_ref[1, q * GROUP + i].astype(F32)
+            real = x_ref[0, q * GROUP + i, :, lanes].astype(F32)
+            imag = x_ref[1, q * GROUP + i, :, lanes].astype(F32)
             power = real * real + imag * imag
             total, width = power, 1
             while width < 2 * HALF_WIDTH:
                 total = total + pltpu.roll(total, width, 1)
                 width *= 2
             total = total + pltpu.roll(power, width, 1)
-            total = pltpu.roll(total, length - HALF_WIDTH, 1)[:, EDGE : EDGE + half]
+            total = pltpu.roll(total, length - HALF_WIDTH, 1)[:, EDGE : length - EDGE]
             gain = lax.rsqrt(total / (2 * HALF_WIDTH + 1) + epsilon)
-            real = (real[:, EDGE : EDGE + half] * gain).astype(jnp.bfloat16)
-            imag = (imag[:, EDGE : EDGE + half] * gain).astype(jnp.bfloat16)
-            for c in range(bands):
-                white[c * groups + q, i, :channels] = real[:, c * BAND : (c + 1) * BAND]
-                white[c * groups + q, i, channels:] = imag[:, c * BAND : (c + 1) * BAND]
+            real = (real[:, EDGE : length - EDGE] * gain).astype(jnp.bfloat16)
+            imag = (imag[:, EDGE : length - EDGE] * gain).astype(jnp.bfloat16)
+            for j in range(count):
+                slot = store(j) * groups + q
+                white[slot, i, :channels] = real[:, j * BAND : (j + 1) * BAND]
+                white[slot, i, channels:] = imag[:, j * BAND : (j + 1) * BAND]
+
+    def whiten_inner(q, carry):
+        load(q).wait()
+        whiten(q, mirrored * BAND, bands - 1, lambda j: j + mirrored * (bands - 2 - 2 * j))
 
         @pl.when(z == 0)
         def _():
@@ -229,19 +284,39 @@
 
         return carry
 
-    lax.fori_loop(0, groups, whiten, 0)
+    def whiten_last(q, carry):
+        whiten(q, (1 - mirrored) * (bands - 1) * BAND, 1, lambda j: bands - 1)
+        s = (bands - 1) * groups + q
+
+        @pl.when(z == 0)
+        def _():
+            first_hop(s).start()
+
+        @pl.when(z == blocks - 1)
+        def _():
+            back_hop(s).start()
+
+        return carry
+
+    lax.fori_loop(0, groups, whiten_inner, 0)
 
     @pl.when(z == 0)
     def _():
-        @pl.loop(groups, bands * groups)
+        @pl.loop(groups, (bands - 1) * groups)
         def _(s):
             first_hop(s).start()
 
     @pl.when(z == blocks - 1)
     def _():
-        @pl.loop(groups, bands * groups)
+        @pl.loop(groups, (bands - 1) * groups)
         def _(s):
             back_hop(s).start()
+
+    @pl.when(takes_edge)
+    def _():
+        edge().wait_recv()
+
+    lax.fori_loop(0, groups, whiten_last, 0)
 
     def transform(buffer, s):
         wide = jnp.concatenate([buffer[s, i] for i in range(GROUP)], axis=1)
@@ -368,15 +443,19 @@
         lax.fori_loop(0, bands, near_band, 0)
 
     def collect(c, carry):
-        mine = pl.ds(pl.multiple_of(m * half + c * BAND, BAND), BAND)
-        theirs = pl.ds(pl.multiple_of((1 - m) * half + c * BAND, BAND), BAND)
+        mine = pl.ds(pl.multiple_of(m * half + place(c) * BAND, BAND), BAND)
+        theirs = pl.ds(pl.multiple_of((1 - m) * half + place(c) * BAND, BAND), BAND)
         out_ref[:, :, mine] = stack[c, :, pl.ds(pl.multiple_of(m * kept, 8), kept)]
         swap(c).wait_recv()
-        out_ref[:, :, theirs] = swapped[c]
+        out_ref[:, :, theirs] = swapped[place(c)]
         swap(c).wait_send()
         return carry
 
     lax.fori_loop(0, bands, collect, 0)
+
+    @pl.when(sends_edge)
+    def _():
+        edge().wait_send()
 
     @pl.when(z < blocks - 1)
     def _():
@@ -410,17 +489,8 @@
 
 def four_block_shards(spectra, counts, owners):
     parts, windows, channels, bins = spectra.shape
-    halves, member = lax.axis_size("pairs"), lax.axis_index("pairs")
-    blocks, z = lax.axis_size("cable"), lax.axis_index("cable")
+    halves, blocks = lax.axis_size("pairs"), lax.axis_size("cable")
     half, points = bins // halves, 2 * channels
-    pad = jnp.zeros((parts, windows, channels, EDGE - HALF_WIDTH), spectra.dtype)
-    padded = with_halo(spectra, (("bins", 3),), HALF_WIDTH)
-    padded = jnp.concatenate([pad, padded, pad], axis=3)
-    padded = lax.dynamic_slice_in_dim(padded, member * half, half + 2 * EDGE, 3)
-    live = jnp.minimum(counts[0], blocks - z)
-    weights = (jnp.arange(REACH + 1) < live).astype(F32)
-    flags = jnp.concatenate([owners[0].astype(F32), weights])
-    flags = jnp.broadcast_to(flags[:, None], (2 * (REACH + 1), BAND))
     forward, inverse = channel_transforms(channels, 1.0 / math.sqrt(windows * channels))
     bands, groups = half // BAND, windows // GROUP
     pieces = bands * groups
@@ -432,9 +502,17 @@
     out = pl.pallas_call(
         stack_kernel,
         out_shape=jax.ShapeDtypeStruct((2, kept, bins), F32),
-        in_specs=[pl.BlockSpec(memory_space=pltpu.VMEM)] * 4,
+        in_specs=[
+            pl.BlockSpec(memory_space=pl.ANY),
+            pl.BlockSpec(memory_space=pltpu.SMEM),
+            pl.BlockSpec(memory_space=pltpu.SMEM),
+            pl.BlockSpec(memory_space=pltpu.VMEM),
+            pl.BlockSpec(memory_space=pltpu.VMEM),
+        ],
         out_specs=pl.BlockSpec(memory_space=pltpu.VMEM),
         scratch_shapes=[
+            pltpu.VMEM((2, windows, channels, half + 2 * EDGE), jnp.bfloat16),
+            pltpu.VMEM((2 * (REACH + 1), BAND), F32),
             block, block, block,
             pltpu.VMEM((pieces, 2 * points, GROUP * BAND), F32),
             pltpu.VMEM((2 * points, GROUP * BAND), F32),
@@ -445,16 +523,17 @@
             pltpu.VMEM((blocks - 1, bands, 2 * points, BAND), F32),
             lags,
             pltpu.VMEM((bands, 2, kept, BAND), F32),
-            pltpu.VMEM(flags.shape, F32),
+            pltpu.VMEM((2 * (REACH + 1), BAND), F32),
             dma((pieces,)), dma((pieces,)), dma((pieces,)), dma((pieces,)),
             dma((bands,)), dma((blocks - 1, bands)),
             dma((bands,)), dma((bands,)), dma((bands,)), dma((bands,)),
             dma((blocks - 1,)), dma((1,)),
+            dma((groups,)), dma((1,)), dma((1,)),
         ],
         compiler_params=pltpu.CompilerParams(
             collective_id=0, has_side_effects=True, vmem_limit_bytes=60 * 1024 * 1024
         ),
-    )(padded, flags, forward, inverse)
+    )(spectra, counts, owners, forward, inverse)
     return out[:, None]
 
 

time: 129 us -> 101 us (0.78)
  local copies, waits for them, and re-layouts: 17.7 us -> 2.52 us
  waiting for transfers between devices: 12.6 us -> 0 us
  Pallas kernels: 90.1 us -> 97.4 us
  starting transfers between devices: 6.2 us -> 0 us
    ppermute x2 -> x0, waiting for transfers between devices: 12.6 us -> none  [the longest x1 8.44 us: with_halo(): before = lax.ppermute(last, axis, up)]
    concatenate x1 -> x0, local copies, waits for them, and re-layouts: 9.11 us -> none  [four_block_shards(): padded = jnp.concatenate([pad, padded, pad], axis=3)]
    pallas_call x1, Pallas kernels: 90.1 us -> 97.4 us  [four_block_shards(): pl.pallas_call(stack_kernel, out_shape=jax.ShapeDtypeStruct((2, kept, bin...]
    ppermute x2 -> x0, starting transfers between devices: 6.2 us -> none  [the longest x1 4.9 us: with_halo(): before = lax.ppermute(last, axis, up)]
    dynamic_slice x1 -> x0, local copies, waits for them, and re-layouts: 3.88 us -> none  [four_block_shards(): padded = lax.dynamic_slice_in_dim(padded, member * half, half + 2 * EDGE, 3)]
    slice x1 -> x0, local copies, waits for them, and re-layouts: 1.46 us -> none  [with_halo(): first = lax.slice_in_dim(x, 0, width, axis=dim)]
  transfers between devices with their start and end apart: 2 -> 0, of which waited for: 2 -> 0; matrix products, arithmetic and copies ran while one was open for 1% -> 0% of each run, Pallas kernels for 0% -> 0%
where the time goes in v2:
time: 101 us
  Pallas kernels  97.4 us (96%)
  local copies, waits for them, and re-layouts  2.52 us (2%)
    pallas_call x1, Pallas kernels, four_block_shards(): pl.pallas_call(stack_kernel, out_shape=jax.ShapeDtypeStruct((2, kept, bin...  97.4 us
    unnamed x1, local copies, waits for them, and re-layouts  2.52 us

profile of v2, /device:TPU:0, one launch (start us, length us, event | category | flops | bytes accessed | tf_op | source)
XLA Modules:
  0.0 100.6 jit_solution(9544191175911973831)
XLA Ops:
  0.7 97.4 %shard_map.55 = f32[2,160,1024]{2,1,0:T(8,128)} custom-call(bf16[2,16,64,1024]{3,2,1,0:T(8,128)(2,1)} %spectra_ref.1, s32[1]{0:T(128)S(6)} %copy.8.counts_ref, s32[1,4]{1,0:T(1,128)} %owners_ref.1, bf16[256,256]{1,0:T(8,128)(2,1)} %constant.4.clone.forward_ref, f32[256,256]{1,0:T(8,128)} %constant.5.clone.inverse_ref), custom_call_target="tpu_custom_call" | custom-call | tf_op jit(solution)/shard_map/pallas_call | solution.py:502
  98.0 2.5 %copy.9 = f32[2,1,160,1024]{3,2,1,0:T(8,128)} copy(f32[2,1,160,1024]{3,2,1,0:T(8,128)} %bitcast.3) | data formatting | bytes 2621440

commit v3 on v2

--- a/solution.py
+++ b/solution.py
@@ -125,7 +125,8 @@
 
 EDGE = 128
 BAND = 128
-GROUP = 4
+GROUP = 2
+EARLY = 2
 F32 = jnp.float32
 MESH = pl.DeviceIdType.MESH
 
@@ -148,7 +149,7 @@
 
 def stack_kernel(
     spectra_ref, counts_ref, owners_ref, forward_ref, inverse_ref, out_ref,
-    x_ref, flag_ref, white, far, back, spec, other, sums, sums_back, stack, piece_out, piece_back, piece_in, arrived, swapped, seen,
+    x_ref, flag_ref, white, far, back, spec, other, third, sums, sums_back, sums_far, stack, piece_out, piece_back, piece_in, arrived, swapped, seen,
     chain_send, chain_recv, back_send, back_recv, piece_send, piece_recv,
     next_send, next_recv, swap_send, swap_recv, flag_send, flag_recv, load_sem, edge_send, edge_recv,
 ):
@@ -181,8 +182,10 @@
     def back_hop(s):
         return remote(white.at[s], back.at[s], back_send.at[s], back_recv.at[s], backward)
 
-    def to_first(c, slot):
-        return remote(piece_out.at[c], piece_in.at[slot, c], piece_send.at[c], piece_recv.at[slot, c], {"cable": 0})
+    def to_first(c, kind, slot):
+        return remote(
+            piece_out.at[kind, c], piece_in.at[slot, c], piece_send.at[kind, c], piece_recv.at[slot, c], {"cable": 0}
+        )
 
     def to_next(c):
         return remote(piece_back.at[c], arrived.at[c], next_send.at[c], next_recv.at[c], onward)
@@ -246,7 +249,7 @@
 
     @pl.when(z == 0)
     def _():
-        for block in range(1, blocks):
+        for block in range(1, blocks - 1):
             flags_to(block).start()
 
     def whiten(q, begin, count, store):
@@ -298,7 +301,18 @@
 
         return carry
 
+    def relay(s):
+        next_hop(s).wait_recv()
+        next_hop(s).start()
+
+    def relay_early(stage):
+        @pl.when(z == 1)
+        def _():
+            for k in range(EARLY):
+                relay(stage * EARLY + k)
+
     lax.fori_loop(0, groups, whiten_inner, 0)
+    relay_early(0)
 
     @pl.when(z == 0)
     def _():
@@ -317,6 +331,7 @@
         edge().wait_recv()
 
     lax.fori_loop(0, groups, whiten_last, 0)
+    relay_early(1)
 
     def transform(buffer, s):
         wide = jnp.concatenate([buffer[s, i] for i in range(GROUP)], axis=1)
@@ -334,21 +349,18 @@
                 gained = gained + (real * real + imag * imag)
             total[k : k + tile] = gained
 
-    def cross_into(total, s, sign):
+    def cross_into(total, near, far):
         for k in range(0, points, tile):
             gained_real = total[k : k + tile]
             gained_imag = total[points + k : points + k + tile]
             for i in range(GROUP):
                 lanes = slice(i * BAND, (i + 1) * BAND)
-                own_real = spec[s, k : k + tile, lanes]
-                own_imag = spec[s, points + k : points + k + tile, lanes]
-                real = other[k : k + tile, lanes]
-                imag = other[points + k : points + k + tile, lanes]
-                gained_real = gained_real + (own_real * real + own_imag * imag)
-                if sign > 0:
-                    gained_imag = gained_imag + (own_imag * real - own_real * imag)
-                else:
-                    gained_imag = gained_imag + (own_real * imag - own_imag * real)
+                near_real = near[k : k + tile, lanes]
+                near_imag = near[points + k : points + k + tile, lanes]
+                far_real = far[k : k + tile, lanes]
+                far_imag = far[points + k : points + k + tile, lanes]
+                gained_real = gained_real + (near_real * far_real + near_imag * far_imag)
+                gained_imag = gained_imag + (near_imag * far_real - near_real * far_imag)
             total[k : k + tile] = gained_real
             total[points + k : points + k + tile] = gained_imag
 
@@ -377,70 +389,100 @@
         return carry
 
     lax.fori_loop(0, bands, own_band, 0)
-
-    @pl.when(z > 0)
+    relay_early(2)
+
+    def counted_far(offset):
+        return seen[offset : offset + 1, :] * seen[REACH + 1 + offset : REACH + 2 + offset, :]
+
+    @pl.when(z == 1)
     def _():
         flags_to(1).wait_recv()
 
-        def far_band(c, carry):
+        def band(c, carry):
+            sums[...] = jnp.zeros_like(sums)
+
+            def step(q, inner):
+                s = c * groups + q
+
+                @pl.when(s >= 3 * EARLY)
+                def _():
+                    relay(s)
+
+                other[...] = transform(far, s)
+                cross_into(sums, other, spec.at[s])
+                return inner
+
+            lax.fori_loop(0, groups, step, 0)
+            piece = lags_of(sums[...], 2 * points)
+            piece_out[0, c] = piece.astype(piece_out.dtype)
+            to_first(c, 0, 0).start()
+            add_piece(c, channels, counted_far(1) * piece)
+            swap(c).start()
+            return carry
+
+        lax.fori_loop(0, bands, band, 0)
+
+    @pl.when(z == 2)
+    def _():
+        flags_to(1).wait_recv()
+
+        def band(c, carry):
             sums[...] = jnp.zeros_like(sums)
             sums_back[...] = jnp.zeros_like(sums_back)
+            sums_far[...] = jnp.zeros_like(sums_far)
 
             def step(q, inner):
                 s = c * groups + q
+                back_hop(s).wait_recv()
+                third[...] = transform(back, s)
+                cross_into(sums_back, spec.at[s], third)
                 next_hop(s).wait_recv()
-
-                @pl.when(z < blocks - 1)
-                def _():
-                    next_hop(s).start()
-
                 other[...] = transform(far, s)
-                cross_into(sums, s, -1)
-
-                @pl.when(z == blocks - 2)
-                def _():
-                    back_hop(s).wait_recv()
-                    other[...] = transform(back, s)
-                    cross_into(sums_back, s, 1)
-
+                cross_into(sums, other, spec.at[s])
+                cross_into(sums_far, other, third)
                 return inner
 
             lax.fori_loop(0, groups, step, 0)
             piece = lags_of(sums[...], 2 * points)
-            piece_out[c] = piece
-            to_first(c, z - 1).start()
-            counted = seen[pl.ds(z, 1), :] * seen[pl.ds(REACH + 1 + z, 1), :]
-            add_piece(c, pl.multiple_of(z * channels, 8), counted * piece)
-
-            @pl.when(z == blocks - 2)
-            def _():
-                piece = flag_ref[REACH + 2 : REACH + 3, :] * lags_of(sums_back[...], 2 * points)
-                sent = flag_ref[1:2, :]
-                piece_back[c] = sent * piece
-                to_next(c).start()
-                add_piece(c, channels, (1.0 - sent) * piece)
-
-            @pl.when(z == blocks - 1)
-            def _():
-                to_next(c).wait_recv()
-                add_piece(c, channels, arrived[c])
-
+            piece_out[0, c] = piece.astype(piece_out.dtype)
+            to_first(c, 0, 1).start()
+            distant = lags_of(sums_far[...], 2 * points)
+            piece_out[1, c] = distant.astype(piece_out.dtype)
+            to_first(c, 1, 2).start()
+            ahead = flag_ref[REACH + 2 : REACH + 3, :] * lags_of(sums_back[...], 2 * points)
+            sent = flag_ref[1:2, :]
+            piece_back[c, 0] = (sent * ahead).astype(piece_back.dtype)
+            piece_back[c, 1] = (counted_far(3) * distant).astype(piece_back.dtype)
+            to_next(c).start()
+            add_piece(c, 2 * channels, counted_far(2) * piece)
+            add_piece(c, channels, (1.0 - sent) * ahead)
             swap(c).start()
             return carry
 
-        lax.fori_loop(0, bands, far_band, 0)
-
-    @pl.when(z == 0)
-    def _():
-        def near_band(c, carry):
-            for offset in range(1, blocks):
-                to_first(c, offset - 1).wait_recv()
-                counted = (1.0 - flag_ref[offset : offset + 1, :]) * flag_ref[REACH + 1 + offset : REACH + 2 + offset, :]
-                add_piece(c, offset * channels, counted * piece_in[offset - 1, c])
+        lax.fori_loop(0, bands, band, 0)
+
+    @pl.when(z == blocks - 1)
+    def _():
+        def band(c, carry):
+            to_next(c).wait_recv()
+            add_piece(c, channels, arrived[c, 0].astype(F32))
+            add_piece(c, 3 * channels, arrived[c, 1].astype(F32))
             swap(c).start()
             return carry
 
-        lax.fori_loop(0, bands, near_band, 0)
+        lax.fori_loop(0, bands, band, 0)
+
+    @pl.when(z == 0)
+    def _():
+        def band(c, carry):
+            for offset in range(1, blocks):
+                to_first(c, 0, offset - 1).wait_recv()
+                counted = (1.0 - flag_ref[offset : offset + 1, :]) * flag_ref[REACH + 1 + offset : REACH + 2 + offset, :]
+                add_piece(c, offset * channels, counted * piece_in[offset - 1, c].astype(F32))
+            swap(c).start()
+            return carry
+
+        lax.fori_loop(0, bands, band, 0)
 
     def collect(c, carry):
         mine = pl.ds(pl.multiple_of(m * half + place(c) * BAND, BAND), BAND)
@@ -457,7 +499,7 @@
     def _():
         edge().wait_send()
 
-    @pl.when(z < blocks - 1)
+    @pl.when(z < 2)
     def _():
         @pl.loop(0, bands * groups)
         def _(s):
@@ -469,21 +511,22 @@
         def _(s):
             back_hop(s).wait_send()
 
-    @pl.when(z > 0)
+    @pl.when((z == 1) | (z == 2))
     def _():
         @pl.loop(0, bands)
         def _(c):
-            to_first(c, z - 1).wait_send()
-
-    @pl.when(z == blocks - 2)
+            to_first(c, 0, z - 1).wait_send()
+
+    @pl.when(z == 2)
     def _():
         @pl.loop(0, bands)
         def _(c):
+            to_first(c, 1, 2).wait_send()
             to_next(c).wait_send()
 
     @pl.when(z == 0)
     def _():
-        for block in range(1, blocks):
+        for block in range(1, blocks - 1):
             flags_to(block).wait_send()
 
 
@@ -497,7 +540,12 @@
     rows = (REACH + 2) * channels
     kept = rows // halves
     block = pltpu.VMEM((pieces, GROUP, points, BAND), jnp.bfloat16)
-    lags = pltpu.VMEM((bands, 2 * points, BAND), F32)
+    spectrum = pltpu.VMEM((2 * points, GROUP * BAND), F32)
+    sums = pltpu.VMEM((2 * points, BAND), F32)
+
+    def lags(lead):
+        return pltpu.VMEM(lead + (2 * points, BAND), jnp.bfloat16)
+
     dma = pltpu.SemaphoreType.DMA
     out = pl.pallas_call(
         stack_kernel,
@@ -515,17 +563,13 @@
             pltpu.VMEM((2 * (REACH + 1), BAND), F32),
             block, block, block,
             pltpu.VMEM((pieces, 2 * points, GROUP * BAND), F32),
-            pltpu.VMEM((2 * points, GROUP * BAND), F32),
-            pltpu.VMEM((2 * points, BAND), F32),
-            pltpu.VMEM((2 * points, BAND), F32),
+            spectrum, spectrum, sums, sums, sums,
             pltpu.VMEM((bands, 2, rows, BAND), F32),
-            lags, lags,
-            pltpu.VMEM((blocks - 1, bands, 2 * points, BAND), F32),
-            lags,
+            lags((2, bands)), lags((bands, 2)), lags((blocks - 1, bands)), lags((bands, 2)),
             pltpu.VMEM((bands, 2, kept, BAND), F32),
             pltpu.VMEM((2 * (REACH + 1), BAND), F32),
             dma((pieces,)), dma((pieces,)), dma((pieces,)), dma((pieces,)),
-            dma((bands,)), dma((blocks - 1, bands)),
+            dma((2, bands)), dma((blocks - 1, bands)),
             dma((bands,)), dma((bands,)), dma((bands,)), dma((bands,)),
             dma((blocks - 1,)), dma((1,)),
             dma((groups,)), dma((1,)), dma((1,)),

time: 101 us -> 81.2 us (0.80)
  Pallas kernels: 97.4 us -> 77.8 us
    pallas_call x1, Pallas kernels: 97.4 us -> 77.8 us  [four_block_shards(): pl.pallas_call(stack_kernel, out_shape=jax.ShapeDtypeStruct((2, kept, bin...]
where the time goes in v3:
time: 81.2 us; the launch traced here: 81 us
  Pallas kernels  77.8 us (96%)
  local copies, waits for them, and re-layouts  2.52 us (3%)
    pallas_call x1, Pallas kernels, four_block_shards(): pl.pallas_call(stack_kernel, out_shape=jax.ShapeDtypeStruct((2, kept, bin...  77.8 us
    unnamed x1, local copies, waits for them, and re-layouts  2.52 us

profile of v3, /device:TPU:0, one launch (start us, length us, event | category | flops | bytes accessed | tf_op | source)
XLA Modules:
  0.0 81.0 jit_solution(13584304751756322764)
XLA Ops:
  0.7 77.8 %shard_map.55 = f32[2,160,1024]{2,1,0:T(8,128)} custom-call(bf16[2,16,64,1024]{3,2,1,0:T(8,128)(2,1)} %spectra_ref.1, s32[1]{0:T(128)S(6)} %copy.8.counts_ref, s32[1,4]{1,0:T(1,128)} %owners_ref.1, bf16[256,256]{1,0:T(8,128)(2,1)} %constant.4.clone.forward_ref, f32[256,256]{1,0:T(8,128)} %constant.5.clone.inverse_ref), custom_call_target="tpu_custom_call" | custom-call | tf_op jit(solution)/shard_map/pallas_call | solution.py:550
  78.5 2.5 %copy.9 = f32[2,1,160,1024]{3,2,1,0:T(8,128)} copy(f32[2,1,160,1024]{3,2,1,0:T(8,128)} %bitcast.3) | data formatting | bytes 2621440

commit v4 on v3

--- a/solution.py
+++ b/solution.py
@@ -126,7 +126,7 @@
 EDGE = 128
 BAND = 128
 GROUP = 2
-EARLY = 2
+EARLY = 3
 F32 = jnp.float32
 MESH = pl.DeviceIdType.MESH
 
@@ -147,8 +147,14 @@
     return jnp.asarray(forward), jnp.asarray(inverse.astype(np.float32))
 
 
+def smoothing_window():
+    distance = np.arange(BAND + 2 * EDGE)[:, None] - (np.arange(BAND)[None, :] + EDGE)
+    ones = (np.abs(distance) <= HALF_WIDTH).astype(jnp.bfloat16)
+    return jnp.asarray(np.concatenate([ones, ones], axis=0))
+
+
 def stack_kernel(
-    spectra_ref, counts_ref, owners_ref, forward_ref, inverse_ref, out_ref,
+    spectra_ref, counts_ref, owners_ref, window_ref, forward_ref, inverse_ref, out_ref,
     x_ref, flag_ref, white, far, back, spec, other, third, sums, sums_back, sums_far, stack, piece_out, piece_back, piece_in, arrived, swapped, seen,
     chain_send, chain_recv, back_send, back_recv, piece_send, piece_recv,
     next_send, next_recv, swap_send, swap_recv, flag_send, flag_recv, load_sem, edge_send, edge_recv,
@@ -253,25 +259,30 @@
             flags_to(block).start()
 
     def whiten(q, begin, count, store):
-        length = count * BAND + 2 * EDGE
-        lanes = pl.ds(pl.multiple_of(begin, BAND), length)
+        lanes = pl.ds(pl.multiple_of(begin, BAND), count * BAND + 2 * EDGE)
+        reals, imags, highs, lows = [], [], [], []
         for i in range(GROUP):
             real = x_ref[0, q * GROUP + i, :, lanes].astype(F32)
             imag = x_ref[1, q * GROUP + i, :, lanes].astype(F32)
             power = real * real + imag * imag
-            total, width = power, 1
-            while width < 2 * HALF_WIDTH:
-                total = total + pltpu.roll(total, width, 1)
-                width *= 2
-            total = total + pltpu.roll(power, width, 1)
-            total = pltpu.roll(total, length - HALF_WIDTH, 1)[:, EDGE : length - EDGE]
+            high = power.astype(jnp.bfloat16)
+            reals.append(real)
+            imags.append(imag)
+            highs.append(high)
+            lows.append((power - high.astype(F32)).astype(jnp.bfloat16))
+        high = jnp.concatenate(highs, axis=0)
+        low = jnp.concatenate(lows, axis=0)
+        for j in range(count):
+            reach = slice(j * BAND, (j + 1) * BAND + 2 * EDGE)
+            terms = jnp.concatenate([high[:, reach], low[:, reach]], axis=1)
+            total = jnp.dot(terms, window_ref[...], preferred_element_type=F32)
             gain = lax.rsqrt(total / (2 * HALF_WIDTH + 1) + epsilon)
-            real = (real[:, EDGE : length - EDGE] * gain).astype(jnp.bfloat16)
-            imag = (imag[:, EDGE : length - EDGE] * gain).astype(jnp.bfloat16)
-            for j in range(count):
-                slot = store(j) * groups + q
-                white[slot, i, :channels] = real[:, j * BAND : (j + 1) * BAND]
-                white[slot, i, channels:] = imag[:, j * BAND : (j + 1) * BAND]
+            here = slice(EDGE + j * BAND, EDGE + (j + 1) * BAND)
+            slot = store(j) * groups + q
+            for i in range(GROUP):
+                rows = gain[i * channels : (i + 1) * channels]
+                white[slot, i, :channels] = (reals[i][:, here] * rows).astype(jnp.bfloat16)
+                white[slot, i, channels:] = (imags[i][:, here] * rows).astype(jnp.bfloat16)
 
     def whiten_inner(q, carry):
         load(q).wait()
@@ -305,14 +316,14 @@
         next_hop(s).wait_recv()
         next_hop(s).start()
 
-    def relay_early(stage):
+    def relay_early(s, count):
         @pl.when(z == 1)
         def _():
-            for k in range(EARLY):
-                relay(stage * EARLY + k)
+            for k in range(count):
+                relay(s + k)
 
     lax.fori_loop(0, groups, whiten_inner, 0)
-    relay_early(0)
+    relay_early(0, 1)
 
     @pl.when(z == 0)
     def _():
@@ -331,7 +342,7 @@
         edge().wait_recv()
 
     lax.fori_loop(0, groups, whiten_last, 0)
-    relay_early(1)
+    relay_early(1, 2)
 
     def transform(buffer, s):
         wide = jnp.concatenate([buffer[s, i] for i in range(GROUP)], axis=1)
@@ -386,10 +397,10 @@
         lax.fori_loop(0, groups, step, 0)
         stack[c] = jnp.zeros(stack.shape[1:], F32)
         add_piece(c, 0, flag_ref[REACH + 1 : REACH + 2, :] * lags_of(sums[:points], points))
+        relay_early(EARLY + c, 1)
         return carry
 
     lax.fori_loop(0, bands, own_band, 0)
-    relay_early(2)
 
     def counted_far(offset):
         return seen[offset : offset + 1, :] * seen[REACH + 1 + offset : REACH + 2 + offset, :]
@@ -404,7 +415,7 @@
             def step(q, inner):
                 s = c * groups + q
 
-                @pl.when(s >= 3 * EARLY)
+                @pl.when(s >= EARLY + bands)
                 def _():
                     relay(s)
 
@@ -554,6 +565,7 @@
             pl.BlockSpec(memory_space=pl.ANY),
             pl.BlockSpec(memory_space=pltpu.SMEM),
             pl.BlockSpec(memory_space=pltpu.SMEM),
+            pl.BlockSpec(memory_space=pltpu.VMEM),
             pl.BlockSpec(memory_space=pltpu.VMEM),
             pl.BlockSpec(memory_space=pltpu.VMEM),
         ],
@@ -577,7 +589,7 @@
         compiler_params=pltpu.CompilerParams(
             collective_id=0, has_side_effects=True, vmem_limit_bytes=60 * 1024 * 1024
         ),
-    )(spectra, counts, owners, forward, inverse)
+    )(spectra, counts, owners, smoothing_window(), forward, inverse)
     return out[:, None]
 
 

time: 81.2 us -> 73.3 us (0.903)
  Pallas kernels: 77.8 us -> 69.9 us
    pallas_call x1, Pallas kernels: 77.8 us -> 69.9 us  [four_block_shards(): pl.pallas_call(stack_kernel, out_shape=jax.ShapeDtypeStruct((2, kept, bin...]
where the time goes in v4:
time: 73.3 us; the launch traced here: 73.1 us
  Pallas kernels  69.9 us (95%)
  local copies, waits for them, and re-layouts  2.52 us (3%)
    pallas_call x1, Pallas kernels, four_block_shards(): pl.pallas_call(stack_kernel, out_shape=jax.ShapeDtypeStruct((2, kept, bin...  69.9 us
    unnamed x1, local copies, waits for them, and re-layouts  2.52 us

profile of v4, /device:TPU:0, one launch (start us, length us, event | category | flops | bytes accessed | tf_op | source)
XLA Modules:
  0.0 73.1 jit_solution(18040418349838716253)
XLA Ops:
  0.7 69.9 %shard_map.64 = f32[2,160,1024]{2,1,0:T(8,128)} custom-call(bf16[2,16,64,1024]{3,2,1,0:T(8,128)(2,1)} %spectra_ref.1, s32[1]{0:T(128)S(6)} %copy.9.counts_ref, s32[1,4]{1,0:T(1,128)} %owners_ref.1, bf16[768,128]{1,0:T(8,128)(2,1)} %constant.8.clone.window_ref, bf16[256,256]{1,0:T(8,128)(2,1)} %constant.6.clone.forward_ref, f32[256,256]{1,0:T(8,128)} %constant.7.clone.inverse_ref), custom_call_target="tpu_custom_call" | custom-call | tf_op jit(solution)/shard_map/pallas_call | solution.py:561
  70.6 2.5 %copy.10 = f32[2,1,160,1024]{3,2,1,0:T(8,128)} copy(f32[2,1,160,1024]{3,2,1,0:T(8,128)} %bitcast.3) | data formatting | bytes 2621440

commit v5 on v4

--- a/solution.py
+++ b/solution.py
@@ -155,7 +155,7 @@
 
 def stack_kernel(
     spectra_ref, counts_ref, owners_ref, window_ref, forward_ref, inverse_ref, out_ref,
-    x_ref, flag_ref, white, far, back, spec, other, third, sums, sums_back, sums_far, stack, piece_out, piece_back, piece_in, arrived, swapped, seen,
+    x_ref, flag_ref, white, far, back, spec, other, third, sums, sums_back, sums_far, stack, near_out, piece_back, near_in, arrived, swapped, seen,
     chain_send, chain_recv, back_send, back_recv, piece_send, piece_recv,
     next_send, next_recv, swap_send, swap_recv, flag_send, flag_recv, load_sem, edge_send, edge_recv,
 ):
@@ -188,9 +188,18 @@
     def back_hop(s):
         return remote(white.at[s], back.at[s], back_send.at[s], back_recv.at[s], backward)
 
-    def to_first(c, kind, slot):
+    def near_rows(source, target):
+        begin, end = source * channels, source * channels + points + (source - 1) * channels
+        return begin, max(begin, target * kept), min(end, (target + 1) * kept)
+
+    def to_first(c, source, target, sender, spot_of):
+        begin, low, high = near_rows(source, target)
         return remote(
-            piece_out.at[kind, c], piece_in.at[slot, c], piece_send.at[kind, c], piece_recv.at[slot, c], {"cable": 0}
+            near_out.at[c, :, low - begin : high - begin],
+            near_in.at[source - 1, sender, spot_of, :, low - target * kept : high - target * kept],
+            piece_send.at[target, c],
+            piece_recv.at[source - 1, sender, spot_of],
+            {"cable": 0, "pairs": target},
         )
 
     def to_next(c):
@@ -237,10 +246,12 @@
     barrier = pltpu.get_barrier_semaphore()
     for step in range(1, blocks):
         pl.semaphore_signal(barrier, inc=1, device_id={"cable": lax.rem(z + step, blocks)}, device_id_type=MESH)
+        across = {"cable": lax.rem(z + step, blocks), "pairs": lax.rem(m + 1, halves)}
+        pl.semaphore_signal(barrier, inc=1, device_id=across, device_id_type=MESH)
     pl.semaphore_signal(barrier, inc=1, device_id=partner, device_id_type=MESH)
     for step in range(1, cuts):
         pl.semaphore_signal(barrier, inc=1, device_id={"bins": lax.rem(x + step, cuts)}, device_id_type=MESH)
-    pl.semaphore_wait(barrier, blocks + cuts - 1)
+    pl.semaphore_wait(barrier, 2 * blocks + cuts - 2)
     sends_edge = (first & (x < cuts - 1)) | (~first & (x > 0))
     takes_edge = (first & (x > 0)) | (~first & (x < cuts - 1))
 
@@ -405,6 +416,9 @@
     def counted_far(offset):
         return seen[offset : offset + 1, :] * seen[REACH + 1 + offset : REACH + 2 + offset, :]
 
+    def counted_near(offset):
+        return (1.0 - seen[offset : offset + 1, :]) * seen[REACH + 1 + offset : REACH + 2 + offset, :]
+
     @pl.when(z == 1)
     def _():
         flags_to(1).wait_recv()
@@ -425,8 +439,11 @@
 
             lax.fori_loop(0, groups, step, 0)
             piece = lags_of(sums[...], 2 * points)
-            piece_out[0, c] = piece.astype(piece_out.dtype)
-            to_first(c, 0, 0).start()
+            near = (counted_near(1) * piece).astype(near_out.dtype)
+            near_out[c, 0, :points] = near[:points]
+            near_out[c, 1, :points] = near[points:]
+            for target in range(2):
+                to_first(c, 1, target, m, place(c)).start()
             add_piece(c, channels, counted_far(1) * piece)
             swap(c).start()
             return carry
@@ -455,11 +472,16 @@
 
             lax.fori_loop(0, groups, step, 0)
             piece = lags_of(sums[...], 2 * points)
-            piece_out[0, c] = piece.astype(piece_out.dtype)
-            to_first(c, 0, 1).start()
             distant = lags_of(sums_far[...], 2 * points)
-            piece_out[1, c] = distant.astype(piece_out.dtype)
-            to_first(c, 1, 2).start()
+            near, beyond = counted_near(2) * piece, counted_near(3) * distant
+            for part in range(2):
+                top = part * points
+                shared = near[top + channels : top + points] + beyond[top : top + channels]
+                near_out[c, part, :channels] = near[top : top + channels].astype(near_out.dtype)
+                near_out[c, part, channels:points] = shared.astype(near_out.dtype)
+                near_out[c, part, points:] = beyond[top + channels : top + points].astype(near_out.dtype)
+            for target in range(2):
+                to_first(c, 2, target, m, place(c)).start()
             ahead = flag_ref[REACH + 2 : REACH + 3, :] * lags_of(sums_back[...], 2 * points)
             sent = flag_ref[1:2, :]
             piece_back[c, 0] = (sent * ahead).astype(piece_back.dtype)
@@ -485,15 +507,9 @@
 
     @pl.when(z == 0)
     def _():
-        def band(c, carry):
-            for offset in range(1, blocks):
-                to_first(c, 0, offset - 1).wait_recv()
-                counted = (1.0 - flag_ref[offset : offset + 1, :]) * flag_ref[REACH + 1 + offset : REACH + 2 + offset, :]
-                add_piece(c, offset * channels, counted * piece_in[offset - 1, c].astype(F32))
+        @pl.loop(0, bands)
+        def _(c):
             swap(c).start()
-            return carry
-
-        lax.fori_loop(0, bands, band, 0)
 
     def collect(c, carry):
         mine = pl.ds(pl.multiple_of(m * half + place(c) * BAND, BAND), BAND)
@@ -506,6 +522,27 @@
 
     lax.fori_loop(0, bands, collect, 0)
 
+    def add_near(target):
+        def band(c, carry):
+            for source in range(1, 3):
+                _, low, high = near_rows(source, target)
+                rows = slice(low - target * kept, high - target * kept)
+                for sender in range(2):
+                    to_first(c, source, target, sender, place(c)).wait_recv()
+                    lanes = pl.ds(pl.multiple_of(sender * half + place(c) * BAND, BAND), BAND)
+                    out_ref[:, rows, lanes] += near_in[source - 1, sender, place(c), :, rows].astype(F32)
+            return carry
+
+        lax.fori_loop(0, bands, band, 0)
+
+    @pl.when((z == 0) & (m == 0))
+    def _():
+        add_near(0)
+
+    @pl.when((z == 0) & (m == 1))
+    def _():
+        add_near(1)
+
     @pl.when(sends_edge)
     def _():
         edge().wait_send()
@@ -522,17 +559,19 @@
         def _(s):
             back_hop(s).wait_send()
 
-    @pl.when((z == 1) | (z == 2))
+    @pl.when(z == 1)
     def _():
         @pl.loop(0, bands)
         def _(c):
-            to_first(c, 0, z - 1).wait_send()
+            for target in range(2):
+                to_first(c, 1, target, m, place(c)).wait_send()
 
     @pl.when(z == 2)
     def _():
         @pl.loop(0, bands)
         def _(c):
-            to_first(c, 1, 2).wait_send()
+            for target in range(2):
+                to_first(c, 2, target, m, place(c)).wait_send()
             to_next(c).wait_send()
 
     @pl.when(z == 0)
@@ -577,11 +616,14 @@
             pltpu.VMEM((pieces, 2 * points, GROUP * BAND), F32),
             spectrum, spectrum, sums, sums, sums,
             pltpu.VMEM((bands, 2, rows, BAND), F32),
-            lags((2, bands)), lags((bands, 2)), lags((blocks - 1, bands)), lags((bands, 2)),
+            pltpu.VMEM((bands, 2, points + channels, BAND), jnp.bfloat16),
+            lags((bands, 2)),
+            pltpu.VMEM((2, halves, bands, 2, kept, BAND), jnp.bfloat16),
+            lags((bands, 2)),
             pltpu.VMEM((bands, 2, kept, BAND), F32),
             pltpu.VMEM((2 * (REACH + 1), BAND), F32),
             dma((pieces,)), dma((pieces,)), dma((pieces,)), dma((pieces,)),
-            dma((2, bands)), dma((blocks - 1, bands)),
+            dma((halves, bands)), dma((2, halves, bands)),
             dma((bands,)), dma((bands,)), dma((bands,)), dma((bands,)),
             dma((blocks - 1,)), dma((1,)),
             dma((groups,)), dma((1,)), dma((1,)),

time: 73.3 us -> 71.1 us (0.970)
  Pallas kernels: 69.9 us -> 67 us
    pallas_call x1, Pallas kernels: 69.9 us -> 67 us  [four_block_shards(): pl.pallas_call(stack_kernel, out_shape=jax.ShapeDtypeStruct((2, kept, bin...]
where the time goes in v5:
time: 71.1 us; the launch traced here: 70.2 us
  Pallas kernels  67 us (94%)
  local copies, waits for them, and re-layouts  2.52 us (4%)
    pallas_call x1, Pallas kernels, four_block_shards(): pl.pallas_call(stack_kernel, out_shape=jax.ShapeDtypeStruct((2, kept, bin...  67 us
    unnamed x1, local copies, waits for them, and re-layouts  2.52 us

profile of v5, /device:TPU:0, one launch (start us, length us, event | category | flops | bytes accessed | tf_op | source)
XLA Modules:
  0.0 70.2 jit_solution(14603677531359665008)
XLA Ops:
  0.7 67.0 %shard_map.64 = f32[2,160,1024]{2,1,0:T(8,128)} custom-call(bf16[2,16,64,1024]{3,2,1,0:T(8,128)(2,1)} %spectra_ref.1, s32[1]{0:T(128)S(6)} %copy.9.counts_ref, s32[1,4]{1,0:T(1,128)} %owners_ref.1, bf16[768,128]{1,0:T(8,128)(2,1)} %constant.8.clone.window_ref, bf16[256,256]{1,0:T(8,128)(2,1)} %constant.6.clone.forward_ref, f32[256,256]{1,0:T(8,128)} %constant.7.clone.inverse_ref), custom_call_target="tpu_custom_call" | custom-call | tf_op jit(solution)/shard_map/pallas_call | solution.py:600
  67.7 2.5 %copy.10 = f32[2,1,160,1024]{3,2,1,0:T(8,128)} copy(f32[2,1,160,1024]{3,2,1,0:T(8,128)} %bitcast.3) | data formatting | bytes 2621440

commit v6 on v5

--- a/solution.py
+++ b/solution.py
@@ -464,6 +464,11 @@
                 back_hop(s).wait_recv()
                 third[...] = transform(back, s)
                 cross_into(sums_back, spec.at[s], third)
+
+                @pl.when(q == groups - 1)
+                def _():
+                    sums_back[...] = flag_ref[REACH + 2 : REACH + 3, :] * lags_of(sums_back[...], 2 * points)
+
                 next_hop(s).wait_recv()
                 other[...] = transform(far, s)
                 cross_into(sums, other, spec.at[s])
@@ -471,8 +476,8 @@
                 return inner
 
             lax.fori_loop(0, groups, step, 0)
-            piece = lags_of(sums[...], 2 * points)
-            distant = lags_of(sums_far[...], 2 * points)
+            both = lags_of(jnp.concatenate([sums[...], sums_far[...]], axis=1), 2 * points)
+            piece, distant = both[:, :BAND], both[:, BAND:]
             near, beyond = counted_near(2) * piece, counted_near(3) * distant
             for part in range(2):
                 top = part * points
@@ -482,7 +487,7 @@
                 near_out[c, part, points:] = beyond[top + channels : top + points].astype(near_out.dtype)
             for target in range(2):
                 to_first(c, 2, target, m, place(c)).start()
-            ahead = flag_ref[REACH + 2 : REACH + 3, :] * lags_of(sums_back[...], 2 * points)
+            ahead = sums_back[...]
             sent = flag_ref[1:2, :]
             piece_back[c, 0] = (sent * ahead).astype(piece_back.dtype)
             piece_back[c, 1] = (counted_far(3) * distant).astype(piece_back.dtype)

time: 71.1 us -> 70.7 us (level)
  no operation moved by 1% of the time
where the time goes in v6:
time: 70.7 us; the launch traced here: 69.9 us
  Pallas kernels  66.7 us (94%)
  local copies, waits for them, and re-layouts  2.52 us (4%)
    pallas_call x1, Pallas kernels, four_block_shards(): pl.pallas_call(stack_kernel, out_shape=jax.ShapeDtypeStruct((2, kept, bin...  66.7 us
    unnamed x1, local copies, waits for them, and re-layouts  2.52 us

profile of v6, /device:TPU:0, one launch (start us, length us, event | category | flops | bytes accessed | tf_op | source)
XLA Modules:
  0.0 69.9 jit_solution(15562942195469875880)
XLA Ops:
  0.7 66.7 %shard_map.64 = f32[2,160,1024]{2,1,0:T(8,128)} custom-call(bf16[2,16,64,1024]{3,2,1,0:T(8,128)(2,1)} %spectra_ref.1, s32[1]{0:T(128)S(6)} %copy.9.counts_ref, s32[1,4]{1,0:T(1,128)} %owners_ref.1, bf16[768,128]{1,0:T(8,128)(2,1)} %constant.8.clone.window_ref, bf16[256,256]{1,0:T(8,128)(2,1)} %constant.6.clone.forward_ref, f32[256,256]{1,0:T(8,128)} %constant.7.clone.inverse_ref), custom_call_target="tpu_custom_call" | custom-call | tf_op jit(solution)/shard_map/pallas_call | solution.py:605
  67.4 2.5 %copy.10 = f32[2,1,160,1024]{3,2,1,0:T(8,128)} copy(f32[2,1,160,1024]{3,2,1,0:T(8,128)} %bitcast.3) | data formatting | bytes 2621440
